TPU v7x, 32 devices: a whole 2x2x4 slice. The times are simulated.
32 devices in a mesh: days: 2 (over x), sta: 16 (over z, y, core).
Axes of the slice: x: 2, y: 2, z: 4, core: 2. Of those that a mesh axis runs over, the one named last changes fastest.
Arguments:
- records: bfloat16 [384, 256, 256], P(('days', 'sta')), parts along dimension 0, may hold values from -330 to 330
- counts: int32 [128, 4], P(('days', 'sta')), parts along dimension 0, may hold values from 0 to 64
- gap_mask: int32 [128, 256], P(('days', 'sta')), parts along dimension 0, may hold values 0 or 1
Outputs:
- cross_spectra: bfloat16 [7, 2, 384, 12, 128], P(None, None, ('days', 'sta')), parts along dimension 2
There are 2 independent parts, one for each index of `days`. A program takes and returns all parts, laid end to end along the dimension named above; each array names one. Nothing has to cross between parts.
All inputs are finite; a program needn't handle non-finite values. No bound on the sum of `gap_mask` on one device may be relied on, other than what follows from the above.
Results may differ from a plain program's by a relative error of at most 0.0062.
Values may be sent and summed in bfloat16 or wider, within the bound.
No kernel may reach another device: no remote copies, remote signals or barrier semaphores. Data moves between devices by JAX's collectives and lax.ppermute only.
A program may use at most 64 MiB of HBM per device.

v0:
```python
import math

import jax
import jax.numpy as jnp
from jax import lax
from jax.experimental import pallas as pl
from jax.experimental.pallas import tpu as pltpu
from jax.sharding import PartitionSpec as P


ROUNDS = 3
LANES = 128
PITCH = 16
SKEW = 8
UNROLL = 16
MIB = 1 << 20
PAIR_COST = pl.CostEstimate(flops=3_000_000_000, transcendentals=0, bytes_accessed=12_000_000)
WHITEN_COST = pl.CostEstimate(flops=2_000_000_000, transcendentals=0, bytes_accessed=8_000_000)

epsilon = 1e-06

NT = (((1,), (1,)), ((), ()))


def fourier_matrix(samples):
    freq_bins = samples // 2
    times_axis = jnp.arange(samples, dtype=jnp.int32)
    bins_axis = jnp.arange(freq_bins, dtype=jnp.int32)
    phase_idx = times_axis[:, None] * bins_axis[None, :] % samples
    angle = 2.0 * math.pi / samples * phase_idx.astype(jnp.float32)
    taper = 0.5 - 0.5 * jnp.cos(2.0 * math.pi / samples * (times_axis.astype(jnp.float32) + 0.5))
    table_re = taper[:, None] * jnp.cos(angle)
    table_im = -taper[:, None] * jnp.sin(angle)
    return jnp.concatenate([table_re.T, table_im.T], axis=0).astype(jnp.bfloat16)


def lane_iota(rows):
    return lax.broadcasted_iota(jnp.int32, (rows, LANES), 1)


def whiten_hour_kernel(hour, counts_ref, records_ref, gap_ref, table_ref, out_ref):
    channels, seg_hour, samples = records_ref.shape
    bins = samples // 2
    stations = gap_ref.shape[0]
    per_tile = LANES // seg_hour
    tile = gap_ref[:, pl.ds(hour // per_tile * LANES, LANES)].astype(jnp.float32)
    turned = pltpu.roll(tile, seg_hour, 1)
    lane = lane_iota(stations)
    low = lane < seg_hour
    doubled = jnp.where(low, tile, turned) if hour % per_tile == 0 else jnp.where(low, turned, tile)
    position = jnp.where(low, lane, lane - seg_hour)
    row = lax.broadcasted_iota(jnp.int32, (bins, LANES), 0)
    low_side = lane_iota(bins) < seg_hour
    slot = jnp.logical_and(row == 0, jnp.logical_not(low_side))
    table = table_ref[...]
    per_station = channels // stations
    valid = [
        jnp.where(
            position[station : station + 1] < counts_ref[station, hour],
            doubled[station : station + 1],
            0.0,
        )
        for station in range(stations)
    ]
    first_half = lane_iota(1) < seg_hour
    for channel in range(0, channels, 2):
        both = jnp.concatenate([records_ref[channel], records_ref[channel + 1]], axis=0)
        spectrum = lax.dot_general(table, both, NT, preferred_element_type=jnp.float32)
        power = jnp.sum(spectrum * spectrum, axis=0, keepdims=True) * (1.0 / samples)
        pair_valid = jnp.where(
            first_half, valid[channel // per_station], valid[(channel + 1) // per_station]
        )
        scaled = spectrum * (lax.rsqrt(power + epsilon) * pair_valid)
        real, imag = scaled[:bins], scaled[bins:]
        one = jnp.where(low_side, real, pltpu.roll(imag, seg_hour, 1))
        two = jnp.where(low_side, pltpu.roll(real, seg_hour, 1), imag)
        for value, at in ((one, channel), (two, channel + 1)):
            value = jnp.where(slot, valid[at // per_station], value)
            out_ref[at] = value.astype(jnp.bfloat16)


def whiten_hour(records, counts, gap_mask, table, hour):
    channels, segments, samples = records.shape
    seg_hour = segments // counts.shape[1]
    bins = samples // 2
    return pl.pallas_call(
        lambda *refs: whiten_hour_kernel(hour, *refs),
        grid=(1,),
        out_shape=jax.ShapeDtypeStruct((channels, bins, LANES), jnp.bfloat16),
        in_specs=[
            pl.BlockSpec(memory_space=pltpu.SMEM),
            pl.BlockSpec((channels, seg_hour, samples), lambda i: (0, hour, 0)),
            pl.BlockSpec(gap_mask.shape, lambda i: (0, 0)),
            pl.BlockSpec(table.shape, lambda i: (0, 0)),
        ],
        out_specs=pl.BlockSpec((channels, bins, LANES), lambda i: (0, 0, 0)),
        cost_estimate=WHITEN_COST,
        compiler_params=pltpu.CompilerParams(vmem_limit_bytes=8 * MIB),
        name="whiten_hour",
    )(counts, records, gap_mask, table)


def pair_hour_kernel(hours, first, last, *refs):
    refs = list(refs)
    distance_ref = refs.pop(0) if last else None
    blocks = [refs.pop(0) for _ in range(ROUNDS + 1)]
    before_ref = None if first else refs.pop(0)
    channels, bins, _ = blocks[0].shape
    half = LANES // 2
    if last:
        kept_ref, *back_refs, wide_ref, acc_ref, back_f32 = refs
    else:
        acc_ref, wide_ref = refs
    pitch = bins + SKEW
    for q, block in enumerate(blocks):
        for channel in range(channels):
            start = (q * channels + channel) * pitch
            wide_ref[start : start + bins, :] = block[channel].astype(jnp.float32)
    for pad in range(PITCH - channels):
        start = (len(blocks) * channels + pad) * pitch
        wide_ref[start : start + bins, :] = jnp.zeros((bins, LANES), jnp.float32)

    def tile_at(q, k):
        return wide_ref[pl.ds(q * channels * pitch + k, PITCH, stride=pitch), :]

    low = lane_iota(PITCH) < half
    zeroth = [tile_at(q, 0) for q in range(len(blocks))]
    valid = [jnp.where(low, pltpu.roll(t, half, 1), t).astype(jnp.bfloat16) for t in zeroth]
    for q, t in enumerate(zeroth):
        wide_ref[pl.ds(q * channels * pitch, PITCH, stride=pitch), :] = jnp.where(low, t, 0.0)
    joint = 0.5 * lax.dot_general(
        valid[0], jnp.concatenate(valid, axis=0), NT, preferred_element_type=jnp.float32
    )
    weight = 1.0 / (hours * jnp.maximum(joint, 1.0))
    weight = jnp.concatenate([weight, weight], axis=0)
    sign = jnp.where(low, 1.0, -1.0)

    def step(k, carry):
        tiles = [tile_at(q, k) for q in range(len(blocks))]
        turned = (pltpu.roll(tiles[0], half, 1) * sign).astype(jnp.bfloat16)
        tiles = [t.astype(jnp.bfloat16) for t in tiles]
        product = weight * lax.dot_general(
            jnp.concatenate([tiles[0], turned], axis=0),
            jnp.concatenate(tiles, axis=0),
            NT,
            preferred_element_type=jnp.float32,
        )
        if not first:
            product = product + before_ref[k]
        acc_ref[k] = product
        return carry

    lax.fori_loop(0, bins, step, 0, unroll=UNROLL)
    if not last:
        return
    for a in range(channels):
        for part in range(2):
            by_bin = acc_ref[:, part * PITCH + a, :].T
            for q in range(len(blocks)):
                rows = by_bin[q * PITCH : q * PITCH + channels]
                place = pl.ds(a * 2 * channels + part, channels, stride=2)
                if q:
                    kept_ref[distance_ref[q - 1], place, :] = rows
                    back_f32[q - 1, pl.ds(2 * a + part, channels, stride=2 * channels), :] = (
                        -rows if part else rows
                    )
                else:
                    kept_ref[0, place, :] = rows
    for q in range(ROUNDS):
        for d in range(ROUNDS):

            @pl.when(distance_ref[q] == d + 1)
            def _():
                back_refs[d][...] = back_f32[q].astype(jnp.bfloat16)


def pair_hour(blocks, before, distances, hours, last):
    channels, bins, lanes = blocks[0].shape
    first = before is None
    acc = (bins, 2 * PITCH, len(blocks) * PITCH)
    rows = 2 * channels * channels
    wide = pltpu.VMEM(
        ((len(blocks) * channels + PITCH - channels) * (bins + SKEW), lanes), jnp.float32
    )
    vmem = pl.BlockSpec(memory_space=pltpu.VMEM)
    args, specs = [], []
    if last:
        args.append(distances)
        specs.append(pl.BlockSpec(memory_space=pltpu.SMEM))
    args += blocks
    specs += [vmem] * len(blocks)
    if not first:
        args.append(before)
        specs.append(vmem)
    if last:
        out_shape = [
            jax.ShapeDtypeStruct((ROUNDS + 1, rows, lanes), jnp.float32),
            *[jax.ShapeDtypeStruct((rows, lanes), jnp.bfloat16)] * ROUNDS,
        ]
        out_specs = [vmem] * (ROUNDS + 1)
        scratch = [
            wide,
            pltpu.VMEM(acc, jnp.float32),
            pltpu.VMEM((ROUNDS, rows, lanes), jnp.float32),
        ]
    else:
        out_shape = jax.ShapeDtypeStruct(acc, jnp.float32)
        out_specs = vmem
        scratch = [wide]
    return pl.pallas_call(
        lambda *refs: pair_hour_kernel(hours, first, last, *refs),
        out_shape=out_shape,
        in_specs=specs,
        out_specs=out_specs,
        scratch_shapes=scratch,
        cost_estimate=PAIR_COST,
        compiler_params=pltpu.CompilerParams(vmem_limit_bytes=16 * MIB),
        name="pair_hour_last" if last else "pair_hour",
    )(*args)


def join_kernel(behind_ref, ahead_ref, *refs):
    from_ahead, from_rear, out_ref = refs[:ROUNDS], refs[ROUNDS : 2 * ROUNDS], refs[-1]
    pairs = out_ref.shape[1]

    def put(slot, value):
        out_ref[slot] = value.reshape(pairs, 2, LANES).astype(jnp.bfloat16)

    put(ROUNDS, behind_ref[0] + ahead_ref[0])
    for d in range(1, ROUNDS + 1):
        put(ROUNDS - d, behind_ref[d] + from_rear[d - 1][...].astype(jnp.float32))
        put(ROUNDS + d, ahead_ref[d] + from_ahead[d - 1][...].astype(jnp.float32))


def join(behind, ahead, from_ahead, from_rear):
    _, rows, lanes = behind.shape
    vmem = pl.BlockSpec(memory_space=pltpu.VMEM)
    return pl.pallas_call(
        join_kernel,
        out_shape=jax.ShapeDtypeStruct((2 * ROUNDS + 1, rows // 2, 2, lanes), jnp.bfloat16),
        in_specs=[vmem] * (2 * ROUNDS + 2),
        out_specs=vmem,
        compiler_params=pltpu.CompilerParams(vmem_limit_bytes=8 * MIB),
        name="join",
    )(behind, ahead, *from_ahead, *from_rear)


LEVEL = 4
DISTANCES = ((3, 1, 2), (1, 3, 2), (3, 2, 1), (1, 2, 3))


def send(value, count, mirrored, *hops):
    levels = count // LEVEL
    pairs = [
        (LEVEL * level + source, LEVEL * ((level + up) % levels) + target)
        for source, target, up in hops
        for level in range(levels)
    ]
    if mirrored:
        pairs = [(count - 1 - source, count - 1 - target) for source, target in pairs]
    return lax.ppermute(value, "sta", pairs)


def shift(value, count, steps):
    pairs = [(source, (source + steps) % count) for source in range(count)]
    return lax.ppermute(value, "sta", pairs)


def fetch_partners(block, count, hour):
    mirrored = hour % 2 == 1
    if count % LEVEL:
        way = -1 if mirrored else 1
        return [shift(block, count, way * steps) for steps in range(1, ROUNDS + 1)]
    far = send(block, count, mirrored, (0, 2, 0), (1, 3, 0), (2, 1, 1), (3, 0, 1))
    near = send(block, count, mirrored, (0, 1, 0), (2, 3, 0), (1, 0, 1), (3, 2, 1))
    other = send(far, count, mirrored, (0, 1, 0), (1, 0, 0), (2, 3, 0), (3, 2, 0))
    return [near, far, other]


def distances_of(count, position, mirrored):
    if count % LEVEL:
        return jnp.arange(1, ROUNDS + 1, dtype=jnp.int32)
    role = position % LEVEL
    return jnp.array(DISTANCES, jnp.int32)[LEVEL - 1 - role if mirrored else role]


def spectra(records, counts, gap_mask):
    channels, _, samples = records.shape
    hours = counts.shape[1]
    bins = samples // 2
    count = lax.axis_size("sta")
    position = lax.axis_index("sta")
    table = fourier_matrix(samples)
    whitened = [whiten_hour(records, counts, gap_mask, table, hour) for hour in range(hours)]
    partners = [fetch_partners(whitened[hour], count, hour) for hour in range(hours)]
    sums = [None, None]
    for hour in range(hours):
        mirrored = hour % 2
        sums[mirrored] = pair_hour(
            [whitened[hour], *partners[hour]],
            sums[mirrored],
            distances_of(count, position, mirrored == 1),
            hours,
            hour + 2 >= hours,
        )
    (behind, *back), (ahead, *forth) = sums
    from_ahead = [shift(back[d - 1], count, -d) for d in range(1, ROUNDS + 1)]
    from_rear = [shift(forth[d - 1], count, d) for d in range(1, ROUNDS + 1)]
    stacked = join(behind, ahead, from_ahead, from_rear)
    stacked = stacked.reshape(2 * ROUNDS + 1, channels, channels, 2, bins)
    return jnp.transpose(stacked, (0, 3, 1, 2, 4))


def solution(mesh):
    in_specs = (P(("days", "sta"), None, None), P(("days", "sta"), None), P(("days", "sta"), None))
    out_specs = P(None, None, ("days", "sta"), None, None)
    return jax.shard_map(
        spectra, mesh=mesh, in_specs=in_specs, out_specs=out_specs, check_vma=False
    )
```

profile of v0, /device:TPU:0, one launch (start us, length us, event | category | flops | bytes accessed | tf_op | source)
XLA Modules:
  0.0 73.2 jit_solution(247724006965674069)
XLA Ops:
  0.1 0.5 multiply_convert_fusion
  0.7 1.4 %copy-done = bf16[12,256,256]{2,1,0:T(8,128)(2,1)S(1)} copy-done((bf16[12,256,256]{2,1,0:T(8,128)(2,1)S(1)}, bf16[12,256,256]{2,1,0:T(8,128)(2,1)}, u32[]{:S(2)}) %copy-start) | copy-done | bytes 1572888
  2.1 0.7 copy-done.2
  2.8 0.7 copy-done.4
  3.4 1.8 %whiten_hour.7.refs_0_ = bf16[12,128,128]{2,1,0:T(8,128)(2,1)} custom-call(s32[4,4]{1,0:T(4,128)S(1)} %copy-done.4, bf16[12,256,256]{2,1,0:T(8,128)(2,1)S(1)} %copy-done, s32[4,256]{1,0:T(4,128)S(1)} %copy-done.2, bf16[256,256]{1,0:T(8,128)(2,1)S(1)} %pad_maximum_fusion.refs_3_), custom_call_target="tpu_custom_call" | custom-call | flops 2000000000 | bytes 8000000 | tf_op jit(solution)/shard_map/whiten_hour/pallas_call | solution.py:86
  5.3 5.5 %collective-permute-start.10 = (bf16[12,128,128]{2,1,0:T(8,128)(2,1)}, bf16[12,128,128]{2,1,0:T(8,128)(2,1)}, u32[]{:S(2)}, u32[]{:S(2)}) collective-permute-start(bf16[12,128,128]{2,1,0:T(8,128)(2,1)} %whiten_hour.7.refs_0_), channel_id=1, source_target_pairs={{15,13},{11,9},{7,5},{3,1},{14,12},{10,8},{6,4},{2,0},{13,10},{9,6... | collective-permute-start | bytes 1179656 | tf_op jit(solution)/shard_map/ppermute | solution.py:261
  10.7 0.7 collective-permute-start.9
  11.5 1.1 %whiten_hour.6.refs_1_ = bf16[12,128,128]{2,1,0:T(8,128)(2,1)S(1)} custom-call(s32[4,4]{1,0:T(4,128)S(1)} %copy-done.4, bf16[12,256,256]{2,1,0:T(8,128)(2,1)S(1)} %copy-done, s32[4,256]{1,0:T(4,128)S(1)} %copy-done.2, bf16[256,256]{1,0:T(8,128)(2,1)S(1)} %pad_maximum_fusion.refs_3_), custom_call_target="tpu_custom_call" | custom-call | flops 2000000000 | bytes 8000000 | tf_op jit(solution)/shard_map/whiten_hour/pallas_call | solution.py:86
  12.6 0.5 collective-permute-start.7
  13.1 1.1 %whiten_hour.5.refs_0_ = bf16[12,128,128]{2,1,0:T(8,128)(2,1)S(1)} custom-call(s32[4,4]{1,0:T(4,128)S(1)} %copy-done.4, bf16[12,256,256]{2,1,0:T(8,128)(2,1)S(1)} %copy-done, s32[4,256]{1,0:T(4,128)S(1)} %copy-done.2, bf16[256,256]{1,0:T(8,128)(2,1)S(1)} %pad_maximum_fusion.refs_3_), custom_call_target="tpu_custom_call" | custom-call | flops 2000000000 | bytes 8000000 | tf_op jit(solution)/shard_map/whiten_hour/pallas_call | solution.py:86
  14.2 1.6 %collective-permute-start.4 = (bf16[12,128,128]{2,1,0:T(8,128)(2,1)S(1)}, bf16[12,128,128]{2,1,0:T(8,128)(2,1)S(1)}, u32[]{:S(2)}, u32[]{:S(2)}) collective-permute-start(bf16[12,128,128]{2,1,0:T(8,128)(2,1)S(1)} %whiten_hour.5.refs_0_), channel_id=1, source_target_pairs={{0,2},{4,6},{8,10},{12,14},{1,3},{5,7},{9,11},{13,15},{2,5},{6,9},... | collective-permute-start | bytes 1179656 | tf_op jit(solution)/shard_map/ppermute | solution.py:261
  15.8 4.7 %collective-permute-done.10.refs_2_ = bf16[12,128,128]{2,1,0:T(8,128)(2,1)} collective-permute-done((bf16[12,128,128]{2,1,0:T(8,128)(2,1)}, bf16[12,128,128]{2,1,0:T(8,128)(2,1)}, u32[]{:S(2)}, u32[]{:S(2)}) %collective-permute-start.10) | collective-permute-done | bytes 393248 | tf_op jit(solution)/shard_map/ppermute | solution.py:261
  20.6 0.1 collective-permute-start.11
  20.6 10.6 %collective-permute-start.6 = (bf16[12,128,128]{2,1,0:T(8,128)(2,1)S(1)}, bf16[12,128,128]{2,1,0:T(8,128)(2,1)}, u32[]{:S(2)}, u32[]{:S(2)}) collective-permute-start(bf16[12,128,128]{2,1,0:T(8,128)(2,1)S(1)} %whiten_hour.6.refs_1_), channel_id=1, source_target_pairs={{15,14},{11,10},{7,6},{3,2},{13,12},{9,8},{5,4},{1,0},{14,11},{10,... | collective-permute-start | bytes 1179656 | tf_op jit(solution)/shard_map/ppermute | solution.py:261
  31.2 1.1 %whiten_hour.4.refs_1_ = bf16[12,128,128]{2,1,0:T(8,128)(2,1)S(1)} custom-call(s32[4,4]{1,0:T(4,128)S(1)} %copy-done.5, bf16[12,256,256]{2,1,0:T(8,128)(2,1)S(1)} %copy-done.1, s32[4,256]{1,0:T(4,128)S(1)} %copy-done.3, bf16[256,256]{1,0:T(8,128)(2,1)S(1)} %pad_maximum_fusion.refs_3_), custom_call_target="tpu_custom_call" | custom-call | flops 2000000000 | bytes 8000000 | tf_op jit(solution)/shard_map/whiten_hour/pallas_call | solution.py:86
  32.4 2.1 %collective-permute-done.7.refs_3_ = bf16[12,128,128]{2,1,0:T(8,128)(2,1)S(1)} collective-permute-done((bf16[12,128,128]{2,1,0:T(8,128)(2,1)S(1)}, bf16[12,128,128]{2,1,0:T(8,128)(2,1)S(1)}, u32[]{:S(2)}, u32[]{:S(2)}) %collective-permute-start.7) | collective-permute-done | bytes 393248 | tf_op jit(solution)/shard_map/ppermute | solution.py:261
  34.5 0.8 %collective-permute-done.4.refs_2_ = bf16[12,128,128]{2,1,0:T(8,128)(2,1)S(1)} collective-permute-done((bf16[12,128,128]{2,1,0:T(8,128)(2,1)S(1)}, bf16[12,128,128]{2,1,0:T(8,128)(2,1)S(1)}, u32[]{:S(2)}, u32[]{:S(2)}) %collective-permute-start.4) | collective-permute-done | bytes 393248 | tf_op jit(solution)/shard_map/ppermute | solution.py:261
  35.3 3.3 %collective-permute-start.5 = (bf16[12,128,128]{2,1,0:T(8,128)(2,1)S(1)}, bf16[12,128,128]{2,1,0:T(8,128)(2,1)S(1)}, u32[]{:S(2)}, u32[]{:S(2)}) collective-permute-start(bf16[12,128,128]{2,1,0:T(8,128)(2,1)S(1)} %collective-permute-done.4.refs_2_), channel_id=1, source_target_pairs={{0,1},{4,5},{8,9},{12,13},{1,0},{5,4},{9,8},{13,12},{2,3},{6,7},{1... | collective-permute-start | bytes 1179656 | tf_op jit(solution)/shard_map/ppermute | solution.py:261
  38.5 4.2 %pair_hour.3.refs_5_ = f32[128,32,64]{2,1,0:T(8,128)S(1)} custom-call(bf16[12,128,128]{2,1,0:T(8,128)(2,1)} %whiten_hour.7.refs_0_, bf16[12,128,128]{2,1,0:T(8,128)(2,1)} %collective-permute-done.9.refs_1_, bf16[12,128,128]{2,1,0:T(8,128)(2,1)} %collective-permute-done.10.refs_2_, bf16[12,128,128]{2,1,0:T(8,128)(2,1)} %collective-permute-done.11.refs_3_), custom_call_target="tpu_custom_call" | custom-call | flops 3000000000 | bytes 12000000 | tf_op jit(solution)/shard_map/pair_hour/pallas_call | solution.py:210
  42.8 2.0 %collective-permute-done.1.refs_3_ = bf16[12,128,128]{2,1,0:T(8,128)(2,1)S(1)} collective-permute-done((bf16[12,128,128]{2,1,0:T(8,128)(2,1)S(1)}, bf16[12,128,128]{2,1,0:T(8,128)(2,1)S(1)}, u32[]{:S(2)}, u32[]{:S(2)}) %collective-permute-start.1) | collective-permute-done | bytes 393248 | tf_op jit(solution)/shard_map/ppermute | solution.py:261
  44.8 4.9 %pair_hour_last.3 = (f32[4,288,128]{2,1,0:T(8,128)S(1)}, bf16[288,128]{1,0:T(8,128)(2,1)S(1)}, bf16[288,128]{1,0:T(8,128)(2,1)S(1)}, bf16[288,128]{1,0:T(8,128)(2,1)S(1)}) custom-call(s32[3]{0:T(128)S(1)} %get-tuple-element.21.refs_0_, bf16[12,128,128]{2,1,0:T(8,128)(2,1)S(1)} %whiten_hour.6.refs_1_, bf16[12,128,128]{2,1,0:T(8,128)(2,1)} %collective-permute-done.6.refs_2_, ...), custom_call_target="tpu_custom_call" | custom-call | flops 3000000000 | bytes 12000000 | tf_op jit(solution)/shard_map/pair_hour_last/pallas_call | solution.py:210
  49.7 0.6 collective-permute-start.15
  50.3 3.5 %collective-permute-start.16 = (bf16[288,128]{1,0:T(8,128)(2,1)S(1)}, bf16[288,128]{1,0:T(8,128)(2,1)S(1)}, u32[]{:S(2)}, u32[]{:S(2)}) collective-permute-start(bf16[288,128]{1,0:T(8,128)(2,1)S(1)} %get-tuple-element.19), channel_id=1, source_target_pairs={{0,2},{1,3},{2,4},{3,5},{4,6},{5,7},{6,8},{7,9},{8,10},{9,11},{10,... | collective-permute-start | bytes 221192 | tf_op jit(solution)/shard_map/ppermute | solution.py:266
  53.8 2.5 %collective-permute-start.17 = (bf16[288,128]{1,0:T(8,128)(2,1)S(1)}, bf16[288,128]{1,0:T(8,128)(2,1)S(1)}, u32[]{:S(2)}, u32[]{:S(2)}) collective-permute-start(bf16[288,128]{1,0:T(8,128)(2,1)S(1)} %get-tuple-element.20), channel_id=1, source_target_pairs={{0,3},{1,4},{2,5},{3,6},{4,7},{5,8},{6,9},{7,10},{8,11},{9,12},{10... | collective-permute-start | bytes 221192 | tf_op jit(solution)/shard_map/ppermute | solution.py:266
  56.2 2.8 %pair_hour.2.refs_5_ = f32[128,32,64]{2,1,0:T(8,128)S(1)} custom-call(bf16[12,128,128]{2,1,0:T(8,128)(2,1)S(1)} %whiten_hour.5.refs_0_, bf16[12,128,128]{2,1,0:T(8,128)(2,1)S(1)} %collective-permute-done.3.refs_1_, bf16[12,128,128]{2,1,0:T(8,128)(2,1)S(1)} %collective-permute-done.4.refs_2_, bf16[12,128,128]{2,1,0:T(8,128)(2,1)S(1)} %collective-permute-done.5.refs_3_), custom_call_target="tpu_custom_call" | custom-call | flops 3000000000 | bytes 12000000 | tf_op jit(solution)/shard_map/pair_hour/pallas_call | solution.py:210
  59.1 4.5 %pair_hour_last.2 = (f32[4,288,128]{2,1,0:T(8,128)S(1)}, bf16[288,128]{1,0:T(8,128)(2,1)S(1)}, bf16[288,128]{1,0:T(8,128)(2,1)S(1)}, bf16[288,128]{1,0:T(8,128)(2,1)S(1)}) custom-call(s32[3]{0:T(128)S(1)} %get-tuple-element.22.refs_0_, bf16[12,128,128]{2,1,0:T(8,128)(2,1)S(1)} %whiten_hour.4.refs_1_, bf16[12,128,128]{2,1,0:T(8,128)(2,1)S(1)} %collective-permute-done.refs_2_, ...), custom_call_target="tpu_custom_call" | custom-call | flops 3000000000 | bytes 12000000 | tf_op jit(solution)/shard_map/pair_hour_last/pallas_call | solution.py:210
  63.6 3.3 %collective-permute-start.12 = (bf16[288,128]{1,0:T(8,128)(2,1)S(1)}, bf16[288,128]{1,0:T(8,128)(2,1)S(1)}, u32[]{:S(2)}, u32[]{:S(2)}) collective-permute-start(bf16[288,128]{1,0:T(8,128)(2,1)S(1)} %get-tuple-element.15), channel_id=1, source_target_pairs={{0,15},{1,0},{2,1},{3,2},{4,3},{5,4},{6,5},{7,6},{8,7},{9,8},{10,9... | collective-permute-start | bytes 221192 | tf_op jit(solution)/shard_map/ppermute | solution.py:266
  66.9 1.2 %collective-permute-start.13 = (bf16[288,128]{1,0:T(8,128)(2,1)S(1)}, bf16[288,128]{1,0:T(8,128)(2,1)S(1)}, u32[]{:S(2)}, u32[]{:S(2)}) collective-permute-start(bf16[288,128]{1,0:T(8,128)(2,1)S(1)} %get-tuple-element.16), channel_id=1, source_target_pairs={{0,14},{1,15},{2,0},{3,1},{4,2},{5,3},{6,4},{7,5},{8,6},{9,7},{10,... | collective-permute-start | bytes 221192 | tf_op jit(solution)/shard_map/ppermute | solution.py:266
  68.1 0.8 %collective-permute-done.12.refs_0_ = bf16[288,128]{1,0:T(8,128)(2,1)S(1)} collective-permute-done((bf16[288,128]{1,0:T(8,128)(2,1)S(1)}, bf16[288,128]{1,0:T(8,128)(2,1)S(1)}, u32[]{:S(2)}, u32[]{:S(2)}) %collective-permute-start.12) | collective-permute-done | bytes 73760 | tf_op jit(solution)/shard_map/ppermute | solution.py:266
  68.9 2.5 %collective-permute-done.13.refs_1_ = bf16[288,128]{1,0:T(8,128)(2,1)S(1)} collective-permute-done((bf16[288,128]{1,0:T(8,128)(2,1)S(1)}, bf16[288,128]{1,0:T(8,128)(2,1)S(1)}, u32[]{:S(2)}, u32[]{:S(2)}) %collective-permute-start.13) | collective-permute-done | bytes 73760 | tf_op jit(solution)/shard_map/ppermute | solution.py:266
  71.4 0.6 collective-permute-done.14.refs_2_
  72.0 1.2 %join.1 = bf16[7,144,2,128]{3,2,1,0:T(2,128)(2,1)} custom-call(f32[4,288,128]{2,1,0:T(8,128)S(1)} %get-tuple-element.13.behind_ref, f32[4,288,128]{2,1,0:T(8,128)S(1)} %get-tuple-element.14.ahead_ref, bf16[288,128]{1,0:T(8,128)(2,1)S(1)} %collective-permute-done.12.refs_0_, bf16[288,128]{1,0:T(8,128)(2,1)S(1)} %collective-permute-done.13.refs_1_, ...), custom_call_target="tpu_custom_call" | custom-call | tf_op jit(solution)/shard_map/join/pallas_call | solution.py:238
  (32 shorter events, 0.3 us)
Async XLA Ops:
  0.7 1.4 %copy-start = (bf16[12,256,256]{2,1,0:T(8,128)(2,1)S(1)}, bf16[12,256,256]{2,1,0:T(8,128)(2,1)}, u32[]{:S(2)}) copy-start(bf16[12,256,256]{2,1,0:T(8,128)(2,1)} %refs_1_.7) | copy-start | bytes 4718596
  2.1 0.7 copy-start.2
  2.8 0.7 copy-start.4
  5.3 15.3 %collective-permute-start.10 = (bf16[12,128,128]{2,1,0:T(8,128)(2,1)}, bf16[12,128,128]{2,1,0:T(8,128)(2,1)}, u32[]{:S(2)}, u32[]{:S(2)}) collective-permute-start(bf16[12,128,128]{2,1,0:T(8,128)(2,1)} %whiten_hour.7.refs_0_), channel_id=1, source_target_pairs={{15,13},{11,9},{7,5},{3,1},{14,12},{10,8},{6,4},{2,0},{13,10},{9,6... | collective-permute-start | bytes 1179656 | tf_op jit(solution)/shard_map/ppermute | solution.py:261
  10.7 21.5 %collective-permute-start.9 = (bf16[12,128,128]{2,1,0:T(8,128)(2,1)}, bf16[12,128,128]{2,1,0:T(8,128)(2,1)}, u32[]{:S(2)}, u32[]{:S(2)}) collective-permute-start(bf16[12,128,128]{2,1,0:T(8,128)(2,1)} %whiten_hour.7.refs_0_), channel_id=1, source_target_pairs={{15,14},{11,10},{7,6},{3,2},{13,12},{9,8},{5,4},{1,0},{14,11},{10,... | collective-permute-start | bytes 1179656 | tf_op jit(solution)/shard_map/ppermute | solution.py:261
  12.5 18.6 %copy-start.1 = (bf16[12,256,256]{2,1,0:T(8,128)(2,1)S(1)}, bf16[12,256,256]{2,1,0:T(8,128)(2,1)}, u32[]{:S(2)}) copy-start(bf16[12,256,256]{2,1,0:T(8,128)(2,1)} %refs_1_.7) | copy-start | bytes 4718596
  12.6 18.6 %copy-start.3 = (s32[4,256]{1,0:T(4,128)S(1)}, s32[4,256]{1,0:T(4,128)}, u32[]{:S(2)}) copy-start(s32[4,256]{1,0:T(4,128)} %refs_2_.7) | copy-start | bytes 12292
  12.6 18.6 %copy-start.5 = (s32[4,4]{1,0:T(4,128)S(1)}, s32[4,4]{1,0:T(4,128)}, u32[]{:S(2)}) copy-start(s32[4,4]{1,0:T(4,128)} %refs_0_.7) | copy-start | bytes 196
  12.6 21.9 %collective-permute-start.7 = (bf16[12,128,128]{2,1,0:T(8,128)(2,1)S(1)}, bf16[12,128,128]{2,1,0:T(8,128)(2,1)S(1)}, u32[]{:S(2)}, u32[]{:S(2)}) collective-permute-start(bf16[12,128,128]{2,1,0:T(8,128)(2,1)S(1)} %whiten_hour.6.refs_1_), channel_id=1, source_target_pairs={{15,13},{11,9},{7,5},{3,1},{14,12},{10,8},{6,4},{2,0},{13,10},{9,6... | collective-permute-start | bytes 1179656 | tf_op jit(solution)/shard_map/ppermute | solution.py:261
  14.2 21.1 %collective-permute-start.4 = (bf16[12,128,128]{2,1,0:T(8,128)(2,1)S(1)}, bf16[12,128,128]{2,1,0:T(8,128)(2,1)S(1)}, u32[]{:S(2)}, u32[]{:S(2)}) collective-permute-start(bf16[12,128,128]{2,1,0:T(8,128)(2,1)S(1)} %whiten_hour.5.refs_0_), channel_id=1, source_target_pairs={{0,2},{4,6},{8,10},{12,14},{1,3},{5,7},{9,11},{13,15},{2,5},{6,9},... | collective-permute-start | bytes 1179656 | tf_op jit(solution)/shard_map/ppermute | solution.py:261
  20.6 14.7 %collective-permute-start.11 = (bf16[12,128,128]{2,1,0:T(8,128)(2,1)}, bf16[12,128,128]{2,1,0:T(8,128)(2,1)}, u32[]{:S(2)}, u32[]{:S(2)}) collective-permute-start(bf16[12,128,128]{2,1,0:T(8,128)(2,1)} %collective-permute-done.10.refs_2_), channel_id=1, source_target_pairs={{15,14},{11,10},{7,6},{3,2},{14,15},{10,11},{6,7},{2,3},{13,12},{9... | collective-permute-start | bytes 1179656 | tf_op jit(solution)/shard_map/ppermute | solution.py:261
  20.6 22.1 %collective-permute-start.6 = (bf16[12,128,128]{2,1,0:T(8,128)(2,1)S(1)}, bf16[12,128,128]{2,1,0:T(8,128)(2,1)}, u32[]{:S(2)}, u32[]{:S(2)}) collective-permute-start(bf16[12,128,128]{2,1,0:T(8,128)(2,1)S(1)} %whiten_hour.6.refs_1_), channel_id=1, source_target_pairs={{15,14},{11,10},{7,6},{3,2},{13,12},{9,8},{5,4},{1,0},{14,11},{10,... | collective-permute-start | bytes 1179656 | tf_op jit(solution)/shard_map/ppermute | solution.py:261
  31.2 3.2 %copy-start.6 = (s32[4,3]{1,0:T(4,128)S(1)}, s32[4,3]{1,0:T(4,128)}, u32[]{:S(2)}) copy-start(s32[4,3]{1,0:T(4,128)} %constant.44.clone) | copy-start | bytes 148
  32.3 12.5 %collective-permute-start.1 = (bf16[12,128,128]{2,1,0:T(8,128)(2,1)S(1)}, bf16[12,128,128]{2,1,0:T(8,128)(2,1)S(1)}, u32[]{:S(2)}, u32[]{:S(2)}) collective-permute-start(bf16[12,128,128]{2,1,0:T(8,128)(2,1)S(1)} %whiten_hour.4.refs_1_), channel_id=1, source_target_pairs={{0,2},{4,6},{8,10},{12,14},{1,3},{5,7},{9,11},{13,15},{2,5},{6,9},... | collective-permute-start | bytes 1179656 | tf_op jit(solution)/shard_map/ppermute | solution.py:261
  34.4 10.4 %collective-permute-start.8 = (bf16[12,128,128]{2,1,0:T(8,128)(2,1)S(1)}, bf16[12,128,128]{2,1,0:T(8,128)(2,1)S(1)}, u32[]{:S(2)}, u32[]{:S(2)}) collective-permute-start(bf16[12,128,128]{2,1,0:T(8,128)(2,1)S(1)} %collective-permute-done.7.refs_3_), channel_id=1, source_target_pairs={{15,14},{11,10},{7,6},{3,2},{14,15},{10,11},{6,7},{2,3},{13,12},{9... | collective-permute-start | bytes 1179656 | tf_op jit(solution)/shard_map/ppermute | solution.py:261
  35.3 15.0 %collective-permute-start.3 = (bf16[12,128,128]{2,1,0:T(8,128)(2,1)S(1)}, bf16[12,128,128]{2,1,0:T(8,128)(2,1)S(1)}, u32[]{:S(2)}, u32[]{:S(2)}) collective-permute-start(bf16[12,128,128]{2,1,0:T(8,128)(2,1)S(1)} %whiten_hour.5.refs_0_), channel_id=1, source_target_pairs={{0,1},{4,5},{8,9},{12,13},{2,3},{6,7},{10,11},{14,15},{1,4},{5,8},... | collective-permute-start | bytes 1179656 | tf_op jit(solution)/shard_map/ppermute | solution.py:261
  35.3 18.5 %collective-permute-start.5 = (bf16[12,128,128]{2,1,0:T(8,128)(2,1)S(1)}, bf16[12,128,128]{2,1,0:T(8,128)(2,1)S(1)}, u32[]{:S(2)}, u32[]{:S(2)}) collective-permute-start(bf16[12,128,128]{2,1,0:T(8,128)(2,1)S(1)} %collective-permute-done.4.refs_2_), channel_id=1, source_target_pairs={{0,1},{4,5},{8,9},{12,13},{1,0},{5,4},{9,8},{13,12},{2,3},{6,7},{1... | collective-permute-start | bytes 1179656 | tf_op jit(solution)/shard_map/ppermute | solution.py:261
  42.7 16.4 %collective-permute-start = (bf16[12,128,128]{2,1,0:T(8,128)(2,1)S(1)}, bf16[12,128,128]{2,1,0:T(8,128)(2,1)S(1)}, u32[]{:S(2)}, u32[]{:S(2)}) collective-permute-start(bf16[12,128,128]{2,1,0:T(8,128)(2,1)S(1)} %whiten_hour.4.refs_1_), channel_id=1, source_target_pairs={{0,1},{4,5},{8,9},{12,13},{2,3},{6,7},{10,11},{14,15},{1,4},{5,8},... | collective-permute-start | bytes 1179656 | tf_op jit(solution)/shard_map/ppermute | solution.py:261
  44.8 14.3 %collective-permute-start.2 = (bf16[12,128,128]{2,1,0:T(8,128)(2,1)S(1)}, bf16[12,128,128]{2,1,0:T(8,128)(2,1)S(1)}, u32[]{:S(2)}, u32[]{:S(2)}) collective-permute-start(bf16[12,128,128]{2,1,0:T(8,128)(2,1)S(1)} %collective-permute-done.1.refs_3_), channel_id=1, source_target_pairs={{0,1},{4,5},{8,9},{12,13},{1,0},{5,4},{9,8},{13,12},{2,3},{6,7},{1... | collective-permute-start | bytes 1179656 | tf_op jit(solution)/shard_map/ppermute | solution.py:261
  49.7 18.4 %collective-permute-start.15 = (bf16[288,128]{1,0:T(8,128)(2,1)S(1)}, bf16[288,128]{1,0:T(8,128)(2,1)S(1)}, u32[]{:S(2)}, u32[]{:S(2)}) collective-permute-start(bf16[288,128]{1,0:T(8,128)(2,1)S(1)} %get-tuple-element.18), channel_id=1, source_target_pairs={{0,1},{1,2},{2,3},{3,4},{4,5},{5,6},{6,7},{7,8},{8,9},{9,10},{10,1... | collective-permute-start | bytes 221192 | tf_op jit(solution)/shard_map/ppermute | solution.py:266
  50.3 17.8 %collective-permute-start.16 = (bf16[288,128]{1,0:T(8,128)(2,1)S(1)}, bf16[288,128]{1,0:T(8,128)(2,1)S(1)}, u32[]{:S(2)}, u32[]{:S(2)}) collective-permute-start(bf16[288,128]{1,0:T(8,128)(2,1)S(1)} %get-tuple-element.19), channel_id=1, source_target_pairs={{0,2},{1,3},{2,4},{3,5},{4,6},{5,7},{6,8},{7,9},{8,10},{9,11},{10,... | collective-permute-start | bytes 221192 | tf_op jit(solution)/shard_map/ppermute | solution.py:266
  53.8 14.3 %collective-permute-start.17 = (bf16[288,128]{1,0:T(8,128)(2,1)S(1)}, bf16[288,128]{1,0:T(8,128)(2,1)S(1)}, u32[]{:S(2)}, u32[]{:S(2)}) collective-permute-start(bf16[288,128]{1,0:T(8,128)(2,1)S(1)} %get-tuple-element.20), channel_id=1, source_target_pairs={{0,3},{1,4},{2,5},{3,6},{4,7},{5,8},{6,9},{7,10},{8,11},{9,12},{10... | collective-permute-start | bytes 221192 | tf_op jit(solution)/shard_map/ppermute | solution.py:266
  63.6 5.3 %collective-permute-start.12 = (bf16[288,128]{1,0:T(8,128)(2,1)S(1)}, bf16[288,128]{1,0:T(8,128)(2,1)S(1)}, u32[]{:S(2)}, u32[]{:S(2)}) collective-permute-start(bf16[288,128]{1,0:T(8,128)(2,1)S(1)} %get-tuple-element.15), channel_id=1, source_target_pairs={{0,15},{1,0},{2,1},{3,2},{4,3},{5,4},{6,5},{7,6},{8,7},{9,8},{10,9... | collective-permute-start | bytes 221192 | tf_op jit(solution)/shard_map/ppermute | solution.py:266
  66.9 4.5 %collective-permute-start.13 = (bf16[288,128]{1,0:T(8,128)(2,1)S(1)}, bf16[288,128]{1,0:T(8,128)(2,1)S(1)}, u32[]{:S(2)}, u32[]{:S(2)}) collective-permute-start(bf16[288,128]{1,0:T(8,128)(2,1)S(1)} %get-tuple-element.16), channel_id=1, source_target_pairs={{0,14},{1,15},{2,0},{3,1},{4,2},{5,3},{6,4},{7,5},{8,6},{9,7},{10,... | collective-permute-start | bytes 221192 | tf_op jit(solution)/shard_map/ppermute | solution.py:266
  68.1 4.0 %collective-permute-start.14 = (bf16[288,128]{1,0:T(8,128)(2,1)S(1)}, bf16[288,128]{1,0:T(8,128)(2,1)S(1)}, u32[]{:S(2)}, u32[]{:S(2)}) collective-permute-start(bf16[288,128]{1,0:T(8,128)(2,1)S(1)} %get-tuple-element.17), channel_id=1, source_target_pairs={{0,13},{1,14},{2,15},{3,0},{4,1},{5,2},{6,3},{7,4},{8,5},{9,6},{10... | collective-permute-start | bytes 221192 | tf_op jit(solution)/shard_map/ppermute | solution.py:266
where the time goes:
time: 73.7 us; the launch traced here: 73.2 us
  starting transfers between devices  33.4 us (45%)
  Pallas kernels  22.6 us (31%)
  waiting for transfers between devices  13.6 us (18%)
  local copies, waits for them, and re-layouts  2.8 us (4%)
    ppermute x12, starting transfers between devices, send(): return lax.ppermute(value, 'sta', pairs)  22.4 us
    pallas_call x4, Pallas kernels, pair_hour(): pl.pallas_call(lambda *refs: pair_hour_kernel(hours, first, last, *refs),...  16.4 us
    ppermute x6, starting transfers between devices, shift(): return lax.ppermute(value, 'sta', pairs)  11 us
    ppermute x12, waiting for transfers between devices, send(): return lax.ppermute(value, 'sta', pairs)  9.63 us
    pallas_call x4, Pallas kernels, whiten_hour(): pl.pallas_call(lambda *refs: whiten_hour_kernel(hour, *refs), grid=(1,),...  5.03 us
    ppermute x6, waiting for transfers between devices, shift(): return lax.ppermute(value, 'sta', pairs)  3.95 us
    unnamed x14, local copies, waits for them, and re-layouts  2.79 us
  transfers between devices with their start and end apart: 18, of which 7 were waited for; matrix products, arithmetic and copies ran while one was open for 0% of the time, Pallas kernels for 27%

commit v1 on v0

--- a/solution.py
+++ b/solution.py
@@ -12,7 +12,7 @@
 LANES = 128
 PITCH = 16
 SKEW = 8
-UNROLL = 16
+UNROLL = 8
 MIB = 1 << 20
 PAIR_COST = pl.CostEstimate(flops=3_000_000_000, transcendentals=0, bytes_accessed=12_000_000)
 WHITEN_COST = pl.CostEstimate(flops=2_000_000_000, transcendentals=0, bytes_accessed=8_000_000)
@@ -38,9 +38,7 @@
     return lax.broadcasted_iota(jnp.int32, (rows, LANES), 1)
 
 
-def whiten_hour_kernel(hour, counts_ref, records_ref, gap_ref, table_ref, out_ref):
-    channels, seg_hour, samples = records_ref.shape
-    bins = samples // 2
+def validity_rows(hour, seg_hour, counts_ref, gap_ref):
     stations = gap_ref.shape[0]
     per_tile = LANES // seg_hour
     tile = gap_ref[:, pl.ds(hour // per_tile * LANES, LANES)].astype(jnp.float32)
@@ -49,12 +47,7 @@
     low = lane < seg_hour
     doubled = jnp.where(low, tile, turned) if hour % per_tile == 0 else jnp.where(low, turned, tile)
     position = jnp.where(low, lane, lane - seg_hour)
-    row = lax.broadcasted_iota(jnp.int32, (bins, LANES), 0)
-    low_side = lane_iota(bins) < seg_hour
-    slot = jnp.logical_and(row == 0, jnp.logical_not(low_side))
-    table = table_ref[...]
-    per_station = channels // stations
-    valid = [
+    return [
         jnp.where(
             position[station : station + 1] < counts_ref[station, hour],
             doubled[station : station + 1],
@@ -62,6 +55,16 @@
         )
         for station in range(stations)
     ]
+
+
+def whiten_block(records_ref, valid, table_ref, out_ref):
+    channels, seg_hour, samples = records_ref.shape
+    bins = samples // 2
+    row = lax.broadcasted_iota(jnp.int32, (bins, LANES), 0)
+    low_side = lane_iota(bins) < seg_hour
+    slot = jnp.logical_and(row == 0, jnp.logical_not(low_side))
+    table = table_ref[...]
+    per_station = channels // len(valid)
     first_half = lane_iota(1) < seg_hour
     for channel in range(0, channels, 2):
         both = jnp.concatenate([records_ref[channel], records_ref[channel + 1]], axis=0)
@@ -79,25 +82,81 @@
             out_ref[at] = value.astype(jnp.bfloat16)
 
 
-def whiten_hour(records, counts, gap_mask, table, hour):
+def whiten_first_kernel(counts_hbm, records_hbm, gap_hbm, table_ref, *refs):
+    out_ref, rest_ref, valid_ref, counts_ref, records_ref, gap_ref, sems = refs
+    seg_hour = records_ref.shape[1]
+    hours = valid_ref.shape[0]
+
+    def hour_of(hour):
+        return records_hbm.at[:, pl.ds(hour * seg_hour, seg_hour), :]
+
+    moves = [(counts_hbm, counts_ref), (gap_hbm, gap_ref), (hour_of(0), records_ref)]
+    moves += [(hour_of(hour), rest_ref.at[hour - 1]) for hour in range(1, hours)]
+    copies = [
+        pltpu.make_async_copy(source, target, sems.at[i])
+        for i, (source, target) in enumerate(moves)
+    ]
+    for copy in copies:
+        copy.start()
+    for copy in copies[:3]:
+        copy.wait()
+    valid = [validity_rows(hour, seg_hour, counts_ref, gap_ref) for hour in range(hours)]
+    for hour in range(1, hours):
+        for station, row in enumerate(valid[hour]):
+            valid_ref[hour, station : station + 1, :] = row
+    whiten_block(records_ref, valid[0], table_ref, out_ref)
+    for copy in copies[3:]:
+        copy.wait()
+
+
+def whiten_first(records, counts, gap_mask, table):
     channels, segments, samples = records.shape
-    seg_hour = segments // counts.shape[1]
-    bins = samples // 2
+    stations, hours = counts.shape
+    seg_hour = segments // hours
+    hbm = pl.BlockSpec(memory_space=pltpu.HBM)
+    vmem = pl.BlockSpec(memory_space=pltpu.VMEM)
+    block = (channels, seg_hour, samples)
+    return pl.pallas_call(
+        whiten_first_kernel,
+        out_shape=[
+            jax.ShapeDtypeStruct((channels, samples // 2, LANES), jnp.bfloat16),
+            jax.ShapeDtypeStruct((hours - 1, *block), records.dtype),
+            jax.ShapeDtypeStruct((hours, stations, LANES), jnp.float32),
+        ],
+        in_specs=[hbm, hbm, hbm, vmem],
+        out_specs=[vmem] * 3,
+        scratch_shapes=[
+            pltpu.SMEM(counts.shape, counts.dtype),
+            pltpu.VMEM(block, records.dtype),
+            pltpu.VMEM(gap_mask.shape, gap_mask.dtype),
+            pltpu.SemaphoreType.DMA((hours + 2,)),
+        ],
+        cost_estimate=WHITEN_COST,
+        compiler_params=pltpu.CompilerParams(vmem_limit_bytes=8 * MIB),
+        name="whiten_first",
+    )(
+        *(pltpu.with_memory_space_constraint(x, pltpu.HBM) for x in (counts, records, gap_mask)),
+        table,
+    )
+
+
+def whiten_hour_kernel(hour, rest_ref, valid_ref, table_ref, out_ref):
+    valid = [valid_ref[hour, station : station + 1, :] for station in range(valid_ref.shape[1])]
+    whiten_block(rest_ref.at[hour - 1], valid, table_ref, out_ref)
+
+
+def whiten_hour(rest, valid, table, hour):
+    _, channels, _, samples = rest.shape
+    vmem = pl.BlockSpec(memory_space=pltpu.VMEM)
     return pl.pallas_call(
         lambda *refs: whiten_hour_kernel(hour, *refs),
-        grid=(1,),
-        out_shape=jax.ShapeDtypeStruct((channels, bins, LANES), jnp.bfloat16),
-        in_specs=[
-            pl.BlockSpec(memory_space=pltpu.SMEM),
-            pl.BlockSpec((channels, seg_hour, samples), lambda i: (0, hour, 0)),
-            pl.BlockSpec(gap_mask.shape, lambda i: (0, 0)),
-            pl.BlockSpec(table.shape, lambda i: (0, 0)),
-        ],
-        out_specs=pl.BlockSpec((channels, bins, LANES), lambda i: (0, 0, 0)),
+        out_shape=jax.ShapeDtypeStruct((channels, samples // 2, LANES), jnp.bfloat16),
+        in_specs=[vmem] * 3,
+        out_specs=vmem,
         cost_estimate=WHITEN_COST,
         compiler_params=pltpu.CompilerParams(vmem_limit_bytes=8 * MIB),
         name="whiten_hour",
-    )(counts, records, gap_mask, table)
+    )(rest, valid, table)
 
 
 def pair_hour_kernel(hours, first, last, *refs):
@@ -129,35 +188,61 @@
     for q, t in enumerate(zeroth):
         wide_ref[pl.ds(q * channels * pitch, PITCH, stride=pitch), :] = jnp.where(low, t, 0.0)
     joint = 0.5 * lax.dot_general(
-        valid[0], jnp.concatenate(valid, axis=0), NT, preferred_element_type=jnp.float32
+        valid[0], jnp.concatenate(valid + valid, axis=0), NT, preferred_element_type=jnp.float32
     )
     weight = 1.0 / (hours * jnp.maximum(joint, 1.0))
     weight = jnp.concatenate([weight, weight], axis=0)
     sign = jnp.where(low, 1.0, -1.0)
+    low_product = lane_iota(2 * PITCH) < half
+    half_bins = bins // 2
 
     def step(k, carry):
-        tiles = [tile_at(q, k) for q in range(len(blocks))]
-        turned = (pltpu.roll(tiles[0], half, 1) * sign).astype(jnp.bfloat16)
-        tiles = [t.astype(jnp.bfloat16) for t in tiles]
-        product = weight * lax.dot_general(
-            jnp.concatenate([tiles[0], turned], axis=0),
-            jnp.concatenate(tiles, axis=0),
+        left, right = [], []
+        for part in range(2):
+            tiles = [tile_at(q, k + part * half_bins) for q in range(len(blocks))]
+            turned = pltpu.roll(tiles[0], half, 1) * sign
+            tiles = [t.astype(jnp.bfloat16) for t in tiles]
+            left += [tiles[0], turned.astype(jnp.bfloat16)]
+            right += tiles
+        product = lax.dot_general(
+            jnp.concatenate(left, axis=0),
+            jnp.concatenate(right, axis=0),
             NT,
             preferred_element_type=jnp.float32,
         )
+        product = weight * jnp.where(low_product, product[: 2 * PITCH], product[2 * PITCH :])
+        place = pl.ds(pl.multiple_of(k * 2 * PITCH, 2 * PITCH), 2 * PITCH)
         if not first:
-            product = product + before_ref[k]
-        acc_ref[k] = product
+            product = product + before_ref[place, :]
+        acc_ref[place, :] = product
         return carry
 
-    lax.fori_loop(0, bins, step, 0, unroll=UNROLL)
+    lax.fori_loop(0, half_bins, step, 0, unroll=UNROLL)
     if not last:
         return
-    for a in range(channels):
-        for part in range(2):
-            by_bin = acc_ref[:, part * PITCH + a, :].T
+    row = lax.broadcasted_iota(jnp.int32, (LANES, LANES), 0)
+    unit = (row == lane_iota(LANES)).astype(jnp.bfloat16)
+    low_half = lane_iota(half) < half
+
+    def finish(a, carry):
+        both = jnp.concatenate(
+            [
+                acc_ref[pl.ds(part * PITCH + a, half_bins, stride=2 * PITCH), :]
+                for part in range(2)
+            ],
+            axis=0,
+        )
+        high = both.astype(jnp.bfloat16)
+        rest = (both - high.astype(jnp.float32)).astype(jnp.bfloat16)
+        by_bin = lax.dot_general(
+            unit, high, NT, preferred_element_type=jnp.float32
+        ) + lax.dot_general(unit, rest, NT, preferred_element_type=jnp.float32)
+        upper, lower = by_bin[:half], by_bin[half:]
+        real = jnp.where(low_half, upper, pltpu.roll(lower, half, 1))
+        imag = jnp.where(low_half, pltpu.roll(upper, half, 1), lower)
+        for part, value in enumerate((real, imag)):
             for q in range(len(blocks)):
-                rows = by_bin[q * PITCH : q * PITCH + channels]
+                rows = value[q * PITCH : q * PITCH + channels]
                 place = pl.ds(a * 2 * channels + part, channels, stride=2)
                 if q:
                     kept_ref[distance_ref[q - 1], place, :] = rows
@@ -166,6 +251,9 @@
                     )
                 else:
                     kept_ref[0, place, :] = rows
+        return carry
+
+    lax.fori_loop(0, channels, finish, 0, unroll=12)
     for q in range(ROUNDS):
         for d in range(ROUNDS):
 
@@ -177,7 +265,7 @@
 def pair_hour(blocks, before, distances, hours, last):
     channels, bins, lanes = blocks[0].shape
     first = before is None
-    acc = (bins, 2 * PITCH, len(blocks) * PITCH)
+    acc = (bins // 2 * 2 * PITCH, lanes)
     rows = 2 * channels * channels
     wide = pltpu.VMEM(
         ((len(blocks) * channels + PITCH - channels) * (bins + SKEW), lanes), jnp.float32
@@ -291,7 +379,8 @@
     count = lax.axis_size("sta")
     position = lax.axis_index("sta")
     table = fourier_matrix(samples)
-    whitened = [whiten_hour(records, counts, gap_mask, table, hour) for hour in range(hours)]
+    first, rest, valid = whiten_first(records, counts, gap_mask, table)
+    whitened = [first] + [whiten_hour(rest, valid, table, hour) for hour in range(1, hours)]
     partners = [fetch_partners(whitened[hour], count, hour) for hour in range(hours)]
     sums = [None, None]
     for hour in range(hours):
@@ -304,8 +393,10 @@
             hour + 2 >= hours,
         )
     (behind, *back), (ahead, *forth) = sums
-    from_ahead = [shift(back[d - 1], count, -d) for d in range(1, ROUNDS + 1)]
-    from_rear = [shift(forth[d - 1], count, d) for d in range(1, ROUNDS + 1)]
+    from_ahead, from_rear = [], []
+    for d in range(1, ROUNDS + 1):
+        from_ahead.append(shift(back[d - 1], count, -d))
+        from_rear.append(shift(forth[d - 1], count, d))
     stacked = join(behind, ahead, from_ahead, from_rear)
     stacked = stacked.reshape(2 * ROUNDS + 1, channels, channels, 2, bins)
     return jnp.transpose(stacked, (0, 3, 1, 2, 4))

time: 73.7 us -> 70 us (0.950)
  Pallas kernels: 22.6 us -> 20.2 us
  local copies, waits for them, and re-layouts: 2.8 us -> 1.28 us
  waiting for transfers between devices: 13.6 us -> 15.1 us
  starting transfers between devices: 33.4 us -> 32.2 us
    pallas_call x4, Pallas kernels: 5.03 us -> 3.11 us  [the longest x1 1.58 us: whiten_first(): pl.pallas_call(whiten_first_kernel, out_shape=[jax.ShapeDtypeStruct((chan...]
    unnamed x14 -> x6, local copies, waits for them, and re-layouts: 2.79 us -> 1.28 us
    ppermute x12, waiting for transfers between devices: 9.63 us -> 11.1 us  [send(): return lax.ppermute(value, 'sta', pairs)]
  transfers between devices with their start and end apart: 18 -> 18, of which waited for: 7 -> 7; matrix products, arithmetic and copies ran while one was open for 0% -> 0% of each run, Pallas kernels for 27% -> 24%
where the time goes in v1:
time: 70 us; the launch traced here: 69.6 us
  starting transfers between devices  32.2 us (46%)
  Pallas kernels  20.2 us (29%)
  waiting for transfers between devices  15.1 us (22%)
  local copies, waits for them, and re-layouts  1.28 us (2%)
    ppermute x12, starting transfers between devices, send(): return lax.ppermute(value, 'sta', pairs)  21.8 us
    pallas_call x4, Pallas kernels, pair_hour(): pl.pallas_call(lambda *refs: pair_hour_kernel(hours, first, last, *refs),...  16 us
    ppermute x12, waiting for transfers between devices, send(): return lax.ppermute(value, 'sta', pairs)  11.1 us
    ppermute x6, starting transfers between devices, shift(): return lax.ppermute(value, 'sta', pairs)  10.4 us
    ppermute x6, waiting for transfers between devices, shift(): return lax.ppermute(value, 'sta', pairs)  3.95 us
    pallas_call x1, Pallas kernels, whiten_first(): pl.pallas_call(whiten_first_kernel, out_shape=[jax.ShapeDtypeStruct((chan...  1.58 us
    pallas_call x3, Pallas kernels, whiten_hour(): pl.pallas_call(lambda *refs: whiten_hour_kernel(hour, *refs), out_shape=j...  1.52 us
  transfers between devices with their start and end apart: 18, of which 7 were waited for; matrix products, arithmetic and copies ran while one was open for 0% of the time, Pallas kernels for 24%

profile of v1, /device:TPU:0, one launch (start us, length us, event | category | flops | bytes accessed | tf_op | source)
XLA Modules:
  0.0 69.6 jit_solution(11009434411609236460)
XLA Ops:
  0.1 0.5 multiply_convert_fusion
  0.7 1.6 %whiten_first.1 = (bf16[12,128,128]{2,1,0:T(8,128)(2,1)S(1)}, bf16[3,12,64,256]{3,2,1,0:T(8,128)(2,1)S(1)}, f32[4,4,128]{2,1,0:T(4,128)S(1)}) custom-call(s32[4,4]{1,0:T(4,128)} %counts_hbm.1, bf16[12,256,256]{2,1,0:T(8,128)(2,1)} %records_hbm.1, s32[4,256]{1,0:T(4,128)} %gap_hbm.1, bf16[256,256]{1,0:T(8,128)(2,1)S(1)} %pad_maximum_fusion.table_ref.refs_2_), custom_call_target="tpu_custom_call" | custom-call | flops 2000000000 | bytes 8000000 | tf_op jit(solution)/shard_map/whiten_first/pallas_call | solution.py:119
  2.3 0.5 whiten_hour.5.refs_0_
  2.8 5.5 %collective-permute-start.10 = (bf16[12,128,128]{2,1,0:T(8,128)(2,1)S(1)}, bf16[12,128,128]{2,1,0:T(8,128)(2,1)S(1)}, u32[]{:S(2)}, u32[]{:S(2)}) collective-permute-start(bf16[12,128,128]{2,1,0:T(8,128)(2,1)S(1)} %whiten_hour.5.refs_0_), channel_id=1, source_target_pairs={{15,13},{11,9},{7,5},{3,1},{14,12},{10,8},{6,4},{2,0},{13,10},{9,6... | collective-permute-start | bytes 1179656 | tf_op jit(solution)/shard_map/ppermute | solution.py:349
  8.3 0.7 %collective-permute-start.9 = (bf16[12,128,128]{2,1,0:T(8,128)(2,1)S(1)}, bf16[12,128,128]{2,1,0:T(8,128)(2,1)S(1)}, u32[]{:S(2)}, u32[]{:S(2)}) collective-permute-start(bf16[12,128,128]{2,1,0:T(8,128)(2,1)S(1)} %whiten_hour.5.refs_0_), channel_id=1, source_target_pairs={{15,14},{11,10},{7,6},{3,2},{13,12},{9,8},{5,4},{1,0},{14,11},{10,... | collective-permute-start | bytes 1179656 | tf_op jit(solution)/shard_map/ppermute | solution.py:349
  9.1 0.5 whiten_hour.4.refs_1_
  9.6 0.5 collective-permute-start.7
  10.1 1.6 %collective-permute-start.4 = (bf16[12,128,128]{2,1,0:T(8,128)(2,1)S(1)}, bf16[12,128,128]{2,1,0:T(8,128)(2,1)S(1)}, u32[]{:S(2)}, u32[]{:S(2)}) collective-permute-start(bf16[12,128,128]{2,1,0:T(8,128)(2,1)S(1)} %get-tuple-element.18.refs_0_), channel_id=1, source_target_pairs={{0,2},{4,6},{8,10},{12,14},{1,3},{5,7},{9,11},{13,15},{2,5},{6,9},... | collective-permute-start | bytes 1179656 | tf_op jit(solution)/shard_map/ppermute | solution.py:349
  11.7 6.2 %collective-permute-done.10.refs_2_ = bf16[12,128,128]{2,1,0:T(8,128)(2,1)S(1)} collective-permute-done((bf16[12,128,128]{2,1,0:T(8,128)(2,1)S(1)}, bf16[12,128,128]{2,1,0:T(8,128)(2,1)S(1)}, u32[]{:S(2)}, u32[]{:S(2)}) %collective-permute-start.10) | collective-permute-done | bytes 393248 | tf_op jit(solution)/shard_map/ppermute | solution.py:349
  17.8 0.1 collective-permute-start.11
  17.9 10.5 %collective-permute-start.6 = (bf16[12,128,128]{2,1,0:T(8,128)(2,1)S(1)}, bf16[12,128,128]{2,1,0:T(8,128)(2,1)S(1)}, u32[]{:S(2)}, u32[]{:S(2)}) collective-permute-start(bf16[12,128,128]{2,1,0:T(8,128)(2,1)S(1)} %whiten_hour.4.refs_1_), channel_id=1, source_target_pairs={{15,14},{11,10},{7,6},{3,2},{13,12},{9,8},{5,4},{1,0},{14,11},{10,... | collective-permute-start | bytes 1179656 | tf_op jit(solution)/shard_map/ppermute | solution.py:349
  28.5 1.3 %copy-done.1 = bf16[3,12,64,256]{3,2,1,0:T(8,128)(2,1)S(1)} copy-done((bf16[3,12,64,256]{3,2,1,0:T(8,128)(2,1)S(1)}, bf16[3,12,64,256]{3,2,1,0:T(8,128)(2,1)}, u32[]{:S(2)}) %copy-start.1) | copy-done | bytes 1179672
  29.7 0.5 whiten_hour.3.refs_1_
  30.3 0.1 collective-permute-start.1
  30.3 1.5 %collective-permute-done.7.refs_3_ = bf16[12,128,128]{2,1,0:T(8,128)(2,1)S(1)} collective-permute-done((bf16[12,128,128]{2,1,0:T(8,128)(2,1)S(1)}, bf16[12,128,128]{2,1,0:T(8,128)(2,1)S(1)}, u32[]{:S(2)}, u32[]{:S(2)}) %collective-permute-start.7) | collective-permute-done | bytes 393248 | tf_op jit(solution)/shard_map/ppermute | solution.py:349
  31.8 0.8 %collective-permute-done.4.refs_2_ = bf16[12,128,128]{2,1,0:T(8,128)(2,1)S(1)} collective-permute-done((bf16[12,128,128]{2,1,0:T(8,128)(2,1)S(1)}, bf16[12,128,128]{2,1,0:T(8,128)(2,1)S(1)}, u32[]{:S(2)}, u32[]{:S(2)}) %collective-permute-start.4) | collective-permute-done | bytes 393248 | tf_op jit(solution)/shard_map/ppermute | solution.py:349
  32.6 2.7 %collective-permute-start.5 = (bf16[12,128,128]{2,1,0:T(8,128)(2,1)S(1)}, bf16[12,128,128]{2,1,0:T(8,128)(2,1)S(1)}, u32[]{:S(2)}, u32[]{:S(2)}) collective-permute-start(bf16[12,128,128]{2,1,0:T(8,128)(2,1)S(1)} %collective-permute-done.4.refs_2_), channel_id=1, source_target_pairs={{0,1},{4,5},{8,9},{12,13},{1,0},{5,4},{9,8},{13,12},{2,3},{6,7},{1... | collective-permute-start | bytes 1179656 | tf_op jit(solution)/shard_map/ppermute | solution.py:349
  35.3 4.0 %pair_hour.3.refs_5_ = f32[2048,128]{1,0:T(8,128)S(1)} custom-call(bf16[12,128,128]{2,1,0:T(8,128)(2,1)S(1)} %whiten_hour.5.refs_0_, bf16[12,128,128]{2,1,0:T(8,128)(2,1)S(1)} %collective-permute-done.9.refs_1_, bf16[12,128,128]{2,1,0:T(8,128)(2,1)S(1)} %collective-permute-done.10.refs_2_, bf16[12,128,128]{2,1,0:T(8,128)(2,1)} %collective-permute-done.11.refs_3_), custom_call_target="tpu_custom_call" | custom-call | flops 3000000000 | bytes 12000000 | tf_op jit(solution)/shard_map/pair_hour/pallas_call | solution.py:298
  39.3 0.1 collective-permute-start
  39.4 2.6 %collective-permute-done.1.refs_3_ = bf16[12,128,128]{2,1,0:T(8,128)(2,1)S(1)} collective-permute-done((bf16[12,128,128]{2,1,0:T(8,128)(2,1)S(1)}, bf16[12,128,128]{2,1,0:T(8,128)(2,1)S(1)}, u32[]{:S(2)}, u32[]{:S(2)}) %collective-permute-start.1) | collective-permute-done | bytes 393248 | tf_op jit(solution)/shard_map/ppermute | solution.py:349
  42.1 4.5 %pair_hour_last.3 = (f32[4,288,128]{2,1,0:T(8,128)S(1)}, bf16[288,128]{1,0:T(8,128)(2,1)S(1)}, bf16[288,128]{1,0:T(8,128)(2,1)S(1)}, bf16[288,128]{1,0:T(8,128)(2,1)S(1)}) custom-call(s32[3]{0:T(128)S(1)} %get-tuple-element.27.refs_0_, bf16[12,128,128]{2,1,0:T(8,128)(2,1)S(1)} %whiten_hour.4.refs_1_, ...), custom_call_target="tpu_custom_call" | custom-call | flops 3000000000 | bytes 12000000 | tf_op jit(solution)/shard_map/pair_hour_last/pallas_call | solution.py:298
  46.6 0.6 collective-permute-start.15
  47.1 2.8 %collective-permute-start.16 = (bf16[288,128]{1,0:T(8,128)(2,1)S(1)}, bf16[288,128]{1,0:T(8,128)(2,1)S(1)}, u32[]{:S(2)}, u32[]{:S(2)}) collective-permute-start(bf16[288,128]{1,0:T(8,128)(2,1)S(1)} %get-tuple-element.25), channel_id=1, source_target_pairs={{0,2},{1,3},{2,4},{3,5},{4,6},{5,7},{6,8},{7,9},{8,10},{9,11},{10,... | collective-permute-start | bytes 221192 | tf_op jit(solution)/shard_map/ppermute | solution.py:354
  50.0 2.5 %collective-permute-start.17 = (bf16[288,128]{1,0:T(8,128)(2,1)S(1)}, bf16[288,128]{1,0:T(8,128)(2,1)S(1)}, u32[]{:S(2)}, u32[]{:S(2)}) collective-permute-start(bf16[288,128]{1,0:T(8,128)(2,1)S(1)} %get-tuple-element.26), channel_id=1, source_target_pairs={{0,3},{1,4},{2,5},{3,6},{4,7},{5,8},{6,9},{7,10},{8,11},{9,12},{10... | collective-permute-start | bytes 221192 | tf_op jit(solution)/shard_map/ppermute | solution.py:354
  52.4 3.0 %pair_hour.2.refs_5_ = f32[2048,128]{1,0:T(8,128)S(1)} custom-call(bf16[12,128,128]{2,1,0:T(8,128)(2,1)S(1)} %get-tuple-element.18.refs_0_, bf16[12,128,128]{2,1,0:T(8,128)(2,1)S(1)} %collective-permute-done.3.refs_1_, bf16[12,128,128]{2,1,0:T(8,128)(2,1)S(1)} %collective-permute-done.4.refs_2_, bf16[12,128,128]{2,1,0:T(8,128)(2,1)S(1)} %collective-permute-done.5.refs_3_), custom_call_target="tpu_custom_call" | custom-call | flops 3000000000 | bytes 12000000 | tf_op jit(solution)/shard_map/pair_hour/pallas_call | solution.py:298
  55.4 4.5 %pair_hour_last.2 = (f32[4,288,128]{2,1,0:T(8,128)S(1)}, bf16[288,128]{1,0:T(8,128)(2,1)S(1)}, bf16[288,128]{1,0:T(8,128)(2,1)S(1)}, bf16[288,128]{1,0:T(8,128)(2,1)S(1)}) custom-call(s32[3]{0:T(128)S(1)} %get-tuple-element.28.refs_0_, bf16[12,128,128]{2,1,0:T(8,128)(2,1)S(1)} %whiten_hour.3.refs_1_, bf16[12,128,128]{2,1,0:T(8,128)(2,1)S(1)} %collective-permute-done.refs_2_, ...), custom_call_target="tpu_custom_call" | custom-call | flops 3000000000 | bytes 12000000 | tf_op jit(solution)/shard_map/pair_hour_last/pallas_call | solution.py:298
  60.0 3.3 %collective-permute-start.12 = (bf16[288,128]{1,0:T(8,128)(2,1)S(1)}, bf16[288,128]{1,0:T(8,128)(2,1)S(1)}, u32[]{:S(2)}, u32[]{:S(2)}) collective-permute-start(bf16[288,128]{1,0:T(8,128)(2,1)S(1)} %get-tuple-element.21), channel_id=1, source_target_pairs={{0,15},{1,0},{2,1},{3,2},{4,3},{5,4},{6,5},{7,6},{8,7},{9,8},{10,9... | collective-permute-start | bytes 221192 | tf_op jit(solution)/shard_map/ppermute | solution.py:354
  63.3 1.2 %collective-permute-start.13 = (bf16[288,128]{1,0:T(8,128)(2,1)S(1)}, bf16[288,128]{1,0:T(8,128)(2,1)S(1)}, u32[]{:S(2)}, u32[]{:S(2)}) collective-permute-start(bf16[288,128]{1,0:T(8,128)(2,1)S(1)} %get-tuple-element.22), channel_id=1, source_target_pairs={{0,14},{1,15},{2,0},{3,1},{4,2},{5,3},{6,4},{7,5},{8,6},{9,7},{10,... | collective-permute-start | bytes 221192 | tf_op jit(solution)/shard_map/ppermute | solution.py:354
  64.5 0.8 %collective-permute-done.12.refs_0_ = bf16[288,128]{1,0:T(8,128)(2,1)S(1)} collective-permute-done((bf16[288,128]{1,0:T(8,128)(2,1)S(1)}, bf16[288,128]{1,0:T(8,128)(2,1)S(1)}, u32[]{:S(2)}, u32[]{:S(2)}) %collective-permute-start.12) | collective-permute-done | bytes 73760 | tf_op jit(solution)/shard_map/ppermute | solution.py:354
  65.3 2.5 %collective-permute-done.13.refs_1_ = bf16[288,128]{1,0:T(8,128)(2,1)S(1)} collective-permute-done((bf16[288,128]{1,0:T(8,128)(2,1)S(1)}, bf16[288,128]{1,0:T(8,128)(2,1)S(1)}, u32[]{:S(2)}, u32[]{:S(2)}) %collective-permute-start.13) | collective-permute-done | bytes 73760 | tf_op jit(solution)/shard_map/ppermute | solution.py:354
  67.8 0.6 collective-permute-done.14.refs_2_
  68.4 1.2 %join.1 = bf16[7,144,2,128]{3,2,1,0:T(2,128)(2,1)} custom-call(f32[4,288,128]{2,1,0:T(8,128)S(1)} %get-tuple-element.19.behind_ref, f32[4,288,128]{2,1,0:T(8,128)S(1)} %get-tuple-element.20.ahead_ref, bf16[288,128]{1,0:T(8,128)(2,1)S(1)} %collective-permute-done.12.refs_0_, bf16[288,128]{1,0:T(8,128)(2,1)S(1)} %collective-permute-done.13.refs_1_, ...), custom_call_target="tpu_custom_call" | custom-call | tf_op jit(solution)/shard_map/join/pallas_call | solution.py:326
  (24 shorter events, 0.2 us)
Async XLA Ops:
  2.3 6.8 %copy-start = (bf16[3,12,64,256]{3,2,1,0:T(8,128)(2,1)}, bf16[3,12,64,256]{3,2,1,0:T(8,128)(2,1)S(1)}, u32[]{:S(2)}) copy-start(bf16[3,12,64,256]{3,2,1,0:T(8,128)(2,1)S(1)} %get-tuple-element.16.refs_0_) | copy-start | bytes 3538948
  2.8 15.0 %collective-permute-start.10 = (bf16[12,128,128]{2,1,0:T(8,128)(2,1)S(1)}, bf16[12,128,128]{2,1,0:T(8,128)(2,1)S(1)}, u32[]{:S(2)}, u32[]{:S(2)}) collective-permute-start(bf16[12,128,128]{2,1,0:T(8,128)(2,1)S(1)} %whiten_hour.5.refs_0_), channel_id=1, source_target_pairs={{15,13},{11,9},{7,5},{3,1},{14,12},{10,8},{6,4},{2,0},{13,10},{9,6... | collective-permute-start | bytes 1179656 | tf_op jit(solution)/shard_map/ppermute | solution.py:349
  8.3 21.9 %collective-permute-start.9 = (bf16[12,128,128]{2,1,0:T(8,128)(2,1)S(1)}, bf16[12,128,128]{2,1,0:T(8,128)(2,1)S(1)}, u32[]{:S(2)}, u32[]{:S(2)}) collective-permute-start(bf16[12,128,128]{2,1,0:T(8,128)(2,1)S(1)} %whiten_hour.5.refs_0_), channel_id=1, source_target_pairs={{15,14},{11,10},{7,6},{3,2},{13,12},{9,8},{5,4},{1,0},{14,11},{10,... | collective-permute-start | bytes 1179656 | tf_op jit(solution)/shard_map/ppermute | solution.py:349
  9.6 22.2 %collective-permute-start.7 = (bf16[12,128,128]{2,1,0:T(8,128)(2,1)S(1)}, bf16[12,128,128]{2,1,0:T(8,128)(2,1)S(1)}, u32[]{:S(2)}, u32[]{:S(2)}) collective-permute-start(bf16[12,128,128]{2,1,0:T(8,128)(2,1)S(1)} %whiten_hour.4.refs_1_), channel_id=1, source_target_pairs={{15,13},{11,9},{7,5},{3,1},{14,12},{10,8},{6,4},{2,0},{13,10},{9,6... | collective-permute-start | bytes 1179656 | tf_op jit(solution)/shard_map/ppermute | solution.py:349
  10.1 22.5 %collective-permute-start.4 = (bf16[12,128,128]{2,1,0:T(8,128)(2,1)S(1)}, bf16[12,128,128]{2,1,0:T(8,128)(2,1)S(1)}, u32[]{:S(2)}, u32[]{:S(2)}) collective-permute-start(bf16[12,128,128]{2,1,0:T(8,128)(2,1)S(1)} %get-tuple-element.18.refs_0_), channel_id=1, source_target_pairs={{0,2},{4,6},{8,10},{12,14},{1,3},{5,7},{9,11},{13,15},{2,5},{6,9},... | collective-permute-start | bytes 1179656 | tf_op jit(solution)/shard_map/ppermute | solution.py:349
  17.8 14.8 %collective-permute-start.11 = (bf16[12,128,128]{2,1,0:T(8,128)(2,1)S(1)}, bf16[12,128,128]{2,1,0:T(8,128)(2,1)}, u32[]{:S(2)}, u32[]{:S(2)}) collective-permute-start(bf16[12,128,128]{2,1,0:T(8,128)(2,1)S(1)} %collective-permute-done.10.refs_2_), channel_id=1, source_target_pairs={{15,14},{11,10},{7,6},{3,2},{14,15},{10,11},{6,7},{2,3},{13,12},{9... | collective-permute-start | bytes 1179656 | tf_op jit(solution)/shard_map/ppermute | solution.py:349
  17.9 21.4 %collective-permute-start.6 = (bf16[12,128,128]{2,1,0:T(8,128)(2,1)S(1)}, bf16[12,128,128]{2,1,0:T(8,128)(2,1)S(1)}, u32[]{:S(2)}, u32[]{:S(2)}) collective-permute-start(bf16[12,128,128]{2,1,0:T(8,128)(2,1)S(1)} %whiten_hour.4.refs_1_), channel_id=1, source_target_pairs={{15,14},{11,10},{7,6},{3,2},{13,12},{9,8},{5,4},{1,0},{14,11},{10,... | collective-permute-start | bytes 1179656 | tf_op jit(solution)/shard_map/ppermute | solution.py:349
  28.5 1.3 %copy-start.1 = (bf16[3,12,64,256]{3,2,1,0:T(8,128)(2,1)S(1)}, bf16[3,12,64,256]{3,2,1,0:T(8,128)(2,1)}, u32[]{:S(2)}) copy-start(bf16[3,12,64,256]{3,2,1,0:T(8,128)(2,1)} %copy-done) | copy-start | bytes 3538948
  29.7 2.1 %copy-start.2 = (s32[4,3]{1,0:T(4,128)S(1)}, s32[4,3]{1,0:T(4,128)}, u32[]{:S(2)}) copy-start(s32[4,3]{1,0:T(4,128)} %constant.44.clone) | copy-start | bytes 148
  30.3 11.8 %collective-permute-start.1 = (bf16[12,128,128]{2,1,0:T(8,128)(2,1)S(1)}, bf16[12,128,128]{2,1,0:T(8,128)(2,1)S(1)}, u32[]{:S(2)}, u32[]{:S(2)}) collective-permute-start(bf16[12,128,128]{2,1,0:T(8,128)(2,1)S(1)} %whiten_hour.3.refs_1_), channel_id=1, source_target_pairs={{0,2},{4,6},{8,10},{12,14},{1,3},{5,7},{9,11},{13,15},{2,5},{6,9},... | collective-permute-start | bytes 1179656 | tf_op jit(solution)/shard_map/ppermute | solution.py:349
  31.8 10.3 %collective-permute-start.8 = (bf16[12,128,128]{2,1,0:T(8,128)(2,1)S(1)}, bf16[12,128,128]{2,1,0:T(8,128)(2,1)S(1)}, u32[]{:S(2)}, u32[]{:S(2)}) collective-permute-start(bf16[12,128,128]{2,1,0:T(8,128)(2,1)S(1)} %collective-permute-done.7.refs_3_), channel_id=1, source_target_pairs={{15,14},{11,10},{7,6},{3,2},{14,15},{10,11},{6,7},{2,3},{13,12},{9... | collective-permute-start | bytes 1179656 | tf_op jit(solution)/shard_map/ppermute | solution.py:349
  32.6 14.5 %collective-permute-start.3 = (bf16[12,128,128]{2,1,0:T(8,128)(2,1)S(1)}, bf16[12,128,128]{2,1,0:T(8,128)(2,1)S(1)}, u32[]{:S(2)}, u32[]{:S(2)}) collective-permute-start(bf16[12,128,128]{2,1,0:T(8,128)(2,1)S(1)} %get-tuple-element.18.refs_0_), channel_id=1, source_target_pairs={{0,1},{4,5},{8,9},{12,13},{2,3},{6,7},{10,11},{14,15},{1,4},{5,8},... | collective-permute-start | bytes 1179656 | tf_op jit(solution)/shard_map/ppermute | solution.py:349
  32.6 17.3 %collective-permute-start.5 = (bf16[12,128,128]{2,1,0:T(8,128)(2,1)S(1)}, bf16[12,128,128]{2,1,0:T(8,128)(2,1)S(1)}, u32[]{:S(2)}, u32[]{:S(2)}) collective-permute-start(bf16[12,128,128]{2,1,0:T(8,128)(2,1)S(1)} %collective-permute-done.4.refs_2_), channel_id=1, source_target_pairs={{0,1},{4,5},{8,9},{12,13},{1,0},{5,4},{9,8},{13,12},{2,3},{6,7},{1... | collective-permute-start | bytes 1179656 | tf_op jit(solution)/shard_map/ppermute | solution.py:349
  39.3 16.1 %collective-permute-start = (bf16[12,128,128]{2,1,0:T(8,128)(2,1)S(1)}, bf16[12,128,128]{2,1,0:T(8,128)(2,1)S(1)}, u32[]{:S(2)}, u32[]{:S(2)}) collective-permute-start(bf16[12,128,128]{2,1,0:T(8,128)(2,1)S(1)} %whiten_hour.3.refs_1_), channel_id=1, source_target_pairs={{0,1},{4,5},{8,9},{12,13},{2,3},{6,7},{10,11},{14,15},{1,4},{5,8},... | collective-permute-start | bytes 1179656 | tf_op jit(solution)/shard_map/ppermute | solution.py:349
  42.1 13.4 %collective-permute-start.2 = (bf16[12,128,128]{2,1,0:T(8,128)(2,1)S(1)}, bf16[12,128,128]{2,1,0:T(8,128)(2,1)S(1)}, u32[]{:S(2)}, u32[]{:S(2)}) collective-permute-start(bf16[12,128,128]{2,1,0:T(8,128)(2,1)S(1)} %collective-permute-done.1.refs_3_), channel_id=1, source_target_pairs={{0,1},{4,5},{8,9},{12,13},{1,0},{5,4},{9,8},{13,12},{2,3},{6,7},{1... | collective-permute-start | bytes 1179656 | tf_op jit(solution)/shard_map/ppermute | solution.py:349
  46.6 17.9 %collective-permute-start.15 = (bf16[288,128]{1,0:T(8,128)(2,1)S(1)}, bf16[288,128]{1,0:T(8,128)(2,1)S(1)}, u32[]{:S(2)}, u32[]{:S(2)}) collective-permute-start(bf16[288,128]{1,0:T(8,128)(2,1)S(1)} %get-tuple-element.24), channel_id=1, source_target_pairs={{0,1},{1,2},{2,3},{3,4},{4,5},{5,6},{6,7},{7,8},{8,9},{9,10},{10,1... | collective-permute-start | bytes 221192 | tf_op jit(solution)/shard_map/ppermute | solution.py:354
  47.1 17.3 %collective-permute-start.16 = (bf16[288,128]{1,0:T(8,128)(2,1)S(1)}, bf16[288,128]{1,0:T(8,128)(2,1)S(1)}, u32[]{:S(2)}, u32[]{:S(2)}) collective-permute-start(bf16[288,128]{1,0:T(8,128)(2,1)S(1)} %get-tuple-element.25), channel_id=1, source_target_pairs={{0,2},{1,3},{2,4},{3,5},{4,6},{5,7},{6,8},{7,9},{8,10},{9,11},{10,... | collective-permute-start | bytes 221192 | tf_op jit(solution)/shard_map/ppermute | solution.py:354
  50.0 14.5 %collective-permute-start.17 = (bf16[288,128]{1,0:T(8,128)(2,1)S(1)}, bf16[288,128]{1,0:T(8,128)(2,1)S(1)}, u32[]{:S(2)}, u32[]{:S(2)}) collective-permute-start(bf16[288,128]{1,0:T(8,128)(2,1)S(1)} %get-tuple-element.26), channel_id=1, source_target_pairs={{0,3},{1,4},{2,5},{3,6},{4,7},{5,8},{6,9},{7,10},{8,11},{9,12},{10... | collective-permute-start | bytes 221192 | tf_op jit(solution)/shard_map/ppermute | solution.py:354
  60.0 5.3 %collective-permute-start.12 = (bf16[288,128]{1,0:T(8,128)(2,1)S(1)}, bf16[288,128]{1,0:T(8,128)(2,1)S(1)}, u32[]{:S(2)}, u32[]{:S(2)}) collective-permute-start(bf16[288,128]{1,0:T(8,128)(2,1)S(1)} %get-tuple-element.21), channel_id=1, source_target_pairs={{0,15},{1,0},{2,1},{3,2},{4,3},{5,4},{6,5},{7,6},{8,7},{9,8},{10,9... | collective-permute-start | bytes 221192 | tf_op jit(solution)/shard_map/ppermute | solution.py:354
  63.3 4.5 %collective-permute-start.13 = (bf16[288,128]{1,0:T(8,128)(2,1)S(1)}, bf16[288,128]{1,0:T(8,128)(2,1)S(1)}, u32[]{:S(2)}, u32[]{:S(2)}) collective-permute-start(bf16[288,128]{1,0:T(8,128)(2,1)S(1)} %get-tuple-element.22), channel_id=1, source_target_pairs={{0,14},{1,15},{2,0},{3,1},{4,2},{5,3},{6,4},{7,5},{8,6},{9,7},{10,... | collective-permute-start | bytes 221192 | tf_op jit(solution)/shard_map/ppermute | solution.py:354
  64.5 4.0 %collective-permute-start.14 = (bf16[288,128]{1,0:T(8,128)(2,1)S(1)}, bf16[288,128]{1,0:T(8,128)(2,1)S(1)}, u32[]{:S(2)}, u32[]{:S(2)}) collective-permute-start(bf16[288,128]{1,0:T(8,128)(2,1)S(1)} %get-tuple-element.23), channel_id=1, source_target_pairs={{0,13},{1,14},{2,15},{3,0},{4,1},{5,2},{6,3},{7,4},{8,5},{9,6},{10... | collective-permute-start | bytes 221192 | tf_op jit(solution)/shard_map/ppermute | solution.py:354

commit v2 on v1

--- a/solution.py
+++ b/solution.py
@@ -12,8 +12,8 @@
 LANES = 128
 PITCH = 16
 SKEW = 8
-UNROLL = 8
 MIB = 1 << 20
+PAIR_LIMIT = 10 * MIB
 PAIR_COST = pl.CostEstimate(flops=3_000_000_000, transcendentals=0, bytes_accessed=12_000_000)
 WHITEN_COST = pl.CostEstimate(flops=2_000_000_000, transcendentals=0, bytes_accessed=8_000_000)
 
@@ -132,7 +132,7 @@
             pltpu.SemaphoreType.DMA((hours + 2,)),
         ],
         cost_estimate=WHITEN_COST,
-        compiler_params=pltpu.CompilerParams(vmem_limit_bytes=8 * MIB),
+        compiler_params=pltpu.CompilerParams(vmem_limit_bytes=4 * MIB),
         name="whiten_first",
     )(
         *(pltpu.with_memory_space_constraint(x, pltpu.HBM) for x in (counts, records, gap_mask)),
@@ -154,14 +154,13 @@
         in_specs=[vmem] * 3,
         out_specs=vmem,
         cost_estimate=WHITEN_COST,
-        compiler_params=pltpu.CompilerParams(vmem_limit_bytes=8 * MIB),
+        compiler_params=pltpu.CompilerParams(vmem_limit_bytes=4 * MIB),
         name="whiten_hour",
     )(rest, valid, table)
 
 
-def pair_hour_kernel(hours, first, last, *refs):
+def pair_hour_kernel(hours, first, last, mirrored, *refs):
     refs = list(refs)
-    distance_ref = refs.pop(0) if last else None
     blocks = [refs.pop(0) for _ in range(ROUNDS + 1)]
     before_ref = None if first else refs.pop(0)
     channels, bins, _ = blocks[0].shape
@@ -217,12 +216,11 @@
         acc_ref[place, :] = product
         return carry
 
-    lax.fori_loop(0, half_bins, step, 0, unroll=UNROLL)
+    lax.fori_loop(0, half_bins, step, 0, unroll=half_bins)
     if not last:
         return
-    row = lax.broadcasted_iota(jnp.int32, (LANES, LANES), 0)
-    unit = (row == lane_iota(LANES)).astype(jnp.bfloat16)
     low_half = lane_iota(half) < half
+    distances = distances_of(mirrored)
 
     def finish(a, carry):
         both = jnp.concatenate(
@@ -232,11 +230,7 @@
             ],
             axis=0,
         )
-        high = both.astype(jnp.bfloat16)
-        rest = (both - high.astype(jnp.float32)).astype(jnp.bfloat16)
-        by_bin = lax.dot_general(
-            unit, high, NT, preferred_element_type=jnp.float32
-        ) + lax.dot_general(unit, rest, NT, preferred_element_type=jnp.float32)
+        by_bin = both.T
         upper, lower = by_bin[:half], by_bin[half:]
         real = jnp.where(low_half, upper, pltpu.roll(lower, half, 1))
         imag = jnp.where(low_half, pltpu.roll(upper, half, 1), lower)
@@ -245,7 +239,7 @@
                 rows = value[q * PITCH : q * PITCH + channels]
                 place = pl.ds(a * 2 * channels + part, channels, stride=2)
                 if q:
-                    kept_ref[distance_ref[q - 1], place, :] = rows
+                    kept_ref[distances[q - 1], place, :] = rows
                     back_f32[q - 1, pl.ds(2 * a + part, channels, stride=2 * channels), :] = (
                         -rows if part else rows
                     )
@@ -257,12 +251,12 @@
     for q in range(ROUNDS):
         for d in range(ROUNDS):
 
-            @pl.when(distance_ref[q] == d + 1)
+            @pl.when(distances[q] == d + 1)
             def _():
                 back_refs[d][...] = back_f32[q].astype(jnp.bfloat16)
 
 
-def pair_hour(blocks, before, distances, hours, last):
+def pair_hour(blocks, before, hours, last, mirrored):
     channels, bins, lanes = blocks[0].shape
     first = before is None
     acc = (bins // 2 * 2 * PITCH, lanes)
@@ -272,9 +266,6 @@
     )
     vmem = pl.BlockSpec(memory_space=pltpu.VMEM)
     args, specs = [], []
-    if last:
-        args.append(distances)
-        specs.append(pl.BlockSpec(memory_space=pltpu.SMEM))
     args += blocks
     specs += [vmem] * len(blocks)
     if not first:
@@ -296,13 +287,13 @@
         out_specs = vmem
         scratch = [wide]
     return pl.pallas_call(
-        lambda *refs: pair_hour_kernel(hours, first, last, *refs),
+        lambda *refs: pair_hour_kernel(hours, first, last, mirrored, *refs),
         out_shape=out_shape,
         in_specs=specs,
         out_specs=out_specs,
         scratch_shapes=scratch,
         cost_estimate=PAIR_COST,
-        compiler_params=pltpu.CompilerParams(vmem_limit_bytes=16 * MIB),
+        compiler_params=pltpu.CompilerParams(vmem_limit_bytes=PAIR_LIMIT),
         name="pair_hour_last" if last else "pair_hour",
     )(*args)
 
@@ -328,7 +319,7 @@
         out_shape=jax.ShapeDtypeStruct((2 * ROUNDS + 1, rows // 2, 2, lanes), jnp.bfloat16),
         in_specs=[vmem] * (2 * ROUNDS + 2),
         out_specs=vmem,
-        compiler_params=pltpu.CompilerParams(vmem_limit_bytes=8 * MIB),
+        compiler_params=pltpu.CompilerParams(vmem_limit_bytes=4 * MIB),
         name="join",
     )(behind, ahead, *from_ahead, *from_rear)
 
@@ -365,11 +356,19 @@
     return [near, far, other]
 
 
-def distances_of(count, position, mirrored):
+def distances_of(mirrored):
+    count = lax.axis_size("sta")
     if count % LEVEL:
-        return jnp.arange(1, ROUNDS + 1, dtype=jnp.int32)
-    role = position % LEVEL
-    return jnp.array(DISTANCES, jnp.int32)[LEVEL - 1 - role if mirrored else role]
+        return list(range(1, ROUNDS + 1))
+    role = lax.rem(lax.axis_index("sta"), LEVEL)
+    role = LEVEL - 1 - role if mirrored else role
+    chosen = []
+    for q in range(ROUNDS):
+        away = jnp.int32(DISTANCES[LEVEL - 1][q])
+        for r in range(LEVEL - 1):
+            away = jnp.where(role == r, DISTANCES[r][q], away)
+        chosen.append(away)
+    return chosen
 
 
 def spectra(records, counts, gap_mask):
@@ -377,7 +376,6 @@
     hours = counts.shape[1]
     bins = samples // 2
     count = lax.axis_size("sta")
-    position = lax.axis_index("sta")
     table = fourier_matrix(samples)
     first, rest, valid = whiten_first(records, counts, gap_mask, table)
     whitened = [first] + [whiten_hour(rest, valid, table, hour) for hour in range(1, hours)]
@@ -388,9 +386,9 @@
         sums[mirrored] = pair_hour(
             [whitened[hour], *partners[hour]],
             sums[mirrored],
-            distances_of(count, position, mirrored == 1),
             hours,
             hour + 2 >= hours,
+            mirrored == 1,
         )
     (behind, *back), (ahead, *forth) = sums
     from_ahead, from_rear = [], []

time: 70 us -> 65.4 us (0.934)
  Pallas kernels: 20.2 us -> 12.3 us
  starting transfers between devices: 32.2 us -> 34.6 us
  waiting for transfers between devices: 15.1 us -> 17.4 us
  local copies, waits for them, and re-layouts: 1.28 us -> 0 us
    pallas_call x4, Pallas kernels: 16 us -> 7.99 us  [pair_hour(): pl.pallas_call(lambda *refs: pair_hour_kernel(hours, first, last, mirrore...]
    ppermute x12, waiting for transfers between devices: 11.1 us -> 13.5 us  [send(): return lax.ppermute(value, 'sta', pairs)]
    ppermute x12, starting transfers between devices: 21.8 us -> 23.2 us  [send(): return lax.ppermute(value, 'sta', pairs)]
    unnamed x6 -> x0, local copies, waits for them, and re-layouts: 1.28 us -> none
    ppermute x6, starting transfers between devices: 10.4 us -> 11.3 us  [shift(): return lax.ppermute(value, 'sta', pairs)]
  transfers between devices with their start and end apart: 18 -> 18, of which waited for: 7 -> 7; matrix products, arithmetic and copies ran while one was open for 0% -> 0% of each run, Pallas kernels for 24% -> 14%
where the time goes in v2:
time: 65.4 us; the launch traced here: 65 us
  starting transfers between devices  34.6 us (53%)
  waiting for transfers between devices  17.4 us (27%)
  Pallas kernels  12.3 us (19%)
    ppermute x12, starting transfers between devices, send(): return lax.ppermute(value, 'sta', pairs)  23.2 us
    ppermute x12, waiting for transfers between devices, send(): return lax.ppermute(value, 'sta', pairs)  13.5 us
    ppermute x6, starting transfers between devices, shift(): return lax.ppermute(value, 'sta', pairs)  11.3 us
    pallas_call x4, Pallas kernels, pair_hour(): pl.pallas_call(lambda *refs: pair_hour_kernel(hours, first, last, mirrore...  7.99 us
    ppermute x6, waiting for transfers between devices, shift(): return lax.ppermute(value, 'sta', pairs)  3.95 us
    pallas_call x1, Pallas kernels, whiten_first(): pl.pallas_call(whiten_first_kernel, out_shape=[jax.ShapeDtypeStruct((chan...  1.59 us
    pallas_call x3, Pallas kernels, whiten_hour(): pl.pallas_call(lambda *refs: whiten_hour_kernel(hour, *refs), out_shape=j...  1.53 us
  transfers between devices with their start and end apart: 18, of which 7 were waited for; matrix products, arithmetic and copies ran while one was open for 0% of the time, Pallas kernels for 14%

profile of v2, /device:TPU:0, one launch (start us, length us, event | category | flops | bytes accessed | tf_op | source)
XLA Modules:
  0.0 65.0 jit_solution(9876821907689206215)
XLA Ops:
  0.1 0.5 multiply_convert_fusion
  0.7 1.6 %whiten_first.1 = (bf16[12,128,128]{2,1,0:T(8,128)(2,1)S(1)}, bf16[3,12,64,256]{3,2,1,0:T(8,128)(2,1)S(1)}, f32[4,4,128]{2,1,0:T(4,128)S(1)}) custom-call(s32[4,4]{1,0:T(4,128)} %counts_hbm.1, bf16[12,256,256]{2,1,0:T(8,128)(2,1)} %records_hbm.1, s32[4,256]{1,0:T(4,128)} %gap_hbm.1, bf16[256,256]{1,0:T(8,128)(2,1)S(1)} %pad_maximum_fusion.table_ref.refs_2_), custom_call_target="tpu_custom_call" | custom-call | flops 2000000000 | bytes 8000000 | tf_op jit(solution)/shard_map/whiten_first/pallas_call | solution.py:119
  2.3 0.5 whiten_hour.5.refs_0_
  2.8 5.5 %collective-permute-start.10 = (bf16[12,128,128]{2,1,0:T(8,128)(2,1)S(1)}, bf16[12,128,128]{2,1,0:T(8,128)(2,1)S(1)}, u32[]{:S(2)}, u32[]{:S(2)}) collective-permute-start(bf16[12,128,128]{2,1,0:T(8,128)(2,1)S(1)} %whiten_hour.5.refs_0_), channel_id=1, source_target_pairs={{15,13},{11,9},{7,5},{3,1},{14,12},{10,8},{6,4},{2,0},{13,10},{9,6... | collective-permute-start | bytes 1179656 | tf_op jit(solution)/shard_map/ppermute | solution.py:340
  8.3 0.7 %collective-permute-start.9 = (bf16[12,128,128]{2,1,0:T(8,128)(2,1)S(1)}, bf16[12,128,128]{2,1,0:T(8,128)(2,1)S(1)}, u32[]{:S(2)}, u32[]{:S(2)}) collective-permute-start(bf16[12,128,128]{2,1,0:T(8,128)(2,1)S(1)} %whiten_hour.5.refs_0_), channel_id=1, source_target_pairs={{15,14},{11,10},{7,6},{3,2},{13,12},{9,8},{5,4},{1,0},{14,11},{10,... | collective-permute-start | bytes 1179656 | tf_op jit(solution)/shard_map/ppermute | solution.py:340
  9.0 0.5 whiten_hour.4.refs_0_
  9.6 0.5 collective-permute-start.7
  10.1 1.6 %collective-permute-start.4 = (bf16[12,128,128]{2,1,0:T(8,128)(2,1)S(1)}, bf16[12,128,128]{2,1,0:T(8,128)(2,1)S(1)}, u32[]{:S(2)}, u32[]{:S(2)}) collective-permute-start(bf16[12,128,128]{2,1,0:T(8,128)(2,1)S(1)} %get-tuple-element.18.refs_0_), channel_id=1, source_target_pairs={{0,2},{4,6},{8,10},{12,14},{1,3},{5,7},{9,11},{13,15},{2,5},{6,9},... | collective-permute-start | bytes 1179656 | tf_op jit(solution)/shard_map/ppermute | solution.py:340
  11.7 6.2 %collective-permute-done.10.refs_2_ = bf16[12,128,128]{2,1,0:T(8,128)(2,1)S(1)} collective-permute-done((bf16[12,128,128]{2,1,0:T(8,128)(2,1)S(1)}, bf16[12,128,128]{2,1,0:T(8,128)(2,1)S(1)}, u32[]{:S(2)}, u32[]{:S(2)}) %collective-permute-start.10) | collective-permute-done | bytes 393248 | tf_op jit(solution)/shard_map/ppermute | solution.py:340
  17.8 0.1 collective-permute-start.11
  17.9 10.5 %collective-permute-start.6 = (bf16[12,128,128]{2,1,0:T(8,128)(2,1)S(1)}, bf16[12,128,128]{2,1,0:T(8,128)(2,1)S(1)}, u32[]{:S(2)}, u32[]{:S(2)}) collective-permute-start(bf16[12,128,128]{2,1,0:T(8,128)(2,1)S(1)} %whiten_hour.4.refs_0_), channel_id=1, source_target_pairs={{15,14},{11,10},{7,6},{3,2},{13,12},{9,8},{5,4},{1,0},{14,11},{10,... | collective-permute-start | bytes 1179656 | tf_op jit(solution)/shard_map/ppermute | solution.py:340
  28.5 0.5 whiten_hour.3.refs_0_
  29.0 0.1 collective-permute-start.1
  29.1 2.7 %collective-permute-done.7.refs_2_ = bf16[12,128,128]{2,1,0:T(8,128)(2,1)S(1)} collective-permute-done((bf16[12,128,128]{2,1,0:T(8,128)(2,1)S(1)}, bf16[12,128,128]{2,1,0:T(8,128)(2,1)S(1)}, u32[]{:S(2)}, u32[]{:S(2)}) %collective-permute-start.7) | collective-permute-done | bytes 393248 | tf_op jit(solution)/shard_map/ppermute | solution.py:340
  31.8 0.8 %collective-permute-done.4.refs_2_ = bf16[12,128,128]{2,1,0:T(8,128)(2,1)S(1)} collective-permute-done((bf16[12,128,128]{2,1,0:T(8,128)(2,1)S(1)}, bf16[12,128,128]{2,1,0:T(8,128)(2,1)S(1)}, u32[]{:S(2)}, u32[]{:S(2)}) %collective-permute-start.4) | collective-permute-done | bytes 393248 | tf_op jit(solution)/shard_map/ppermute | solution.py:340
  32.6 4.1 %collective-permute-start.5 = (bf16[12,128,128]{2,1,0:T(8,128)(2,1)S(1)}, bf16[12,128,128]{2,1,0:T(8,128)(2,1)S(1)}, u32[]{:S(2)}, u32[]{:S(2)}) collective-permute-start(bf16[12,128,128]{2,1,0:T(8,128)(2,1)S(1)} %collective-permute-done.4.refs_2_), channel_id=1, source_target_pairs={{0,1},{4,5},{8,9},{12,13},{1,0},{5,4},{9,8},{13,12},{2,3},{6,7},{1... | collective-permute-start | bytes 1179656 | tf_op jit(solution)/shard_map/ppermute | solution.py:340
  36.7 1.6 %pair_hour.3.refs_4_ = f32[2048,128]{1,0:T(8,128)S(1)} custom-call(bf16[12,128,128]{2,1,0:T(8,128)(2,1)S(1)} %whiten_hour.5.refs_0_, bf16[12,128,128]{2,1,0:T(8,128)(2,1)S(1)} %collective-permute-done.9.refs_1_, bf16[12,128,128]{2,1,0:T(8,128)(2,1)S(1)} %collective-permute-done.10.refs_2_, bf16[12,128,128]{2,1,0:T(8,128)(2,1)S(1)} %collective-permute-done.11.refs_3_), custom_call_target="tpu_custom_call" | custom-call | flops 3000000000 | bytes 12000000 | tf_op jit(solution)/shard_map/pair_hour/pallas_call | solution.py:289
  38.3 0.1 collective-permute-start
  38.4 3.7 %collective-permute-done.1.refs_2_ = bf16[12,128,128]{2,1,0:T(8,128)(2,1)S(1)} collective-permute-done((bf16[12,128,128]{2,1,0:T(8,128)(2,1)S(1)}, bf16[12,128,128]{2,1,0:T(8,128)(2,1)S(1)}, u32[]{:S(2)}, u32[]{:S(2)}) %collective-permute-start.1) | collective-permute-done | bytes 393248 | tf_op jit(solution)/shard_map/ppermute | solution.py:340
  42.1 2.4 %pair_hour_last.3 = (f32[4,288,128]{2,1,0:T(8,128)S(1)}, bf16[288,128]{1,0:T(8,128)(2,1)S(1)}, bf16[288,128]{1,0:T(8,128)(2,1)S(1)}, bf16[288,128]{1,0:T(8,128)(2,1)S(1)}) custom-call(bf16[12,128,128]{2,1,0:T(8,128)(2,1)S(1)} %whiten_hour.4.refs_0_, bf16[12,128,128]{2,1,0:T(8,128)(2,1)S(1)} %collective-permute-done.6.refs_1_, ...), custom_call_target="tpu_custom_call" | custom-call | flops 3000000000 | bytes 12000000 | tf_op jit(solution)/shard_map/pair_hour_last/pallas_call | solution.py:289
  44.5 0.6 collective-permute-start.15
  45.1 3.8 %collective-permute-start.16 = (bf16[288,128]{1,0:T(8,128)(2,1)S(1)}, bf16[288,128]{1,0:T(8,128)(2,1)S(1)}, u32[]{:S(2)}, u32[]{:S(2)}) collective-permute-start(bf16[288,128]{1,0:T(8,128)(2,1)S(1)} %get-tuple-element.25), channel_id=1, source_target_pairs={{0,2},{1,3},{2,4},{3,5},{4,6},{5,7},{6,8},{7,9},{8,10},{9,11},{10,... | collective-permute-start | bytes 221192 | tf_op jit(solution)/shard_map/ppermute | solution.py:345
  48.9 2.5 %collective-permute-start.17 = (bf16[288,128]{1,0:T(8,128)(2,1)S(1)}, bf16[288,128]{1,0:T(8,128)(2,1)S(1)}, u32[]{:S(2)}, u32[]{:S(2)}) collective-permute-start(bf16[288,128]{1,0:T(8,128)(2,1)S(1)} %get-tuple-element.26), channel_id=1, source_target_pairs={{0,3},{1,4},{2,5},{3,6},{4,7},{5,8},{6,9},{7,10},{8,11},{9,12},{10... | collective-permute-start | bytes 221192 | tf_op jit(solution)/shard_map/ppermute | solution.py:345
  51.3 1.5 %pair_hour.2.refs_4_ = f32[2048,128]{1,0:T(8,128)S(1)} custom-call(bf16[12,128,128]{2,1,0:T(8,128)(2,1)S(1)} %get-tuple-element.18.refs_0_, bf16[12,128,128]{2,1,0:T(8,128)(2,1)S(1)} %collective-permute-done.3.refs_1_, bf16[12,128,128]{2,1,0:T(8,128)(2,1)S(1)} %collective-permute-done.4.refs_2_, bf16[12,128,128]{2,1,0:T(8,128)(2,1)S(1)} %collective-permute-done.5.refs_3_), custom_call_target="tpu_custom_call" | custom-call | flops 3000000000 | bytes 12000000 | tf_op jit(solution)/shard_map/pair_hour/pallas_call | solution.py:289
  52.9 0.0 collective-permute-done.2.refs_3_
  52.9 2.4 %pair_hour_last.2 = (f32[4,288,128]{2,1,0:T(8,128)S(1)}, bf16[288,128]{1,0:T(8,128)(2,1)S(1)}, bf16[288,128]{1,0:T(8,128)(2,1)S(1)}, bf16[288,128]{1,0:T(8,128)(2,1)S(1)}) custom-call(bf16[12,128,128]{2,1,0:T(8,128)(2,1)S(1)} %whiten_hour.3.refs_0_, bf16[12,128,128]{2,1,0:T(8,128)(2,1)S(1)} %collective-permute-done.refs_1_, ...), custom_call_target="tpu_custom_call" | custom-call | flops 3000000000 | bytes 12000000 | tf_op jit(solution)/shard_map/pair_hour_last/pallas_call | solution.py:289
  55.4 3.3 %collective-permute-start.12 = (bf16[288,128]{1,0:T(8,128)(2,1)S(1)}, bf16[288,128]{1,0:T(8,128)(2,1)S(1)}, u32[]{:S(2)}, u32[]{:S(2)}) collective-permute-start(bf16[288,128]{1,0:T(8,128)(2,1)S(1)} %get-tuple-element.21), channel_id=1, source_target_pairs={{0,15},{1,0},{2,1},{3,2},{4,3},{5,4},{6,5},{7,6},{8,7},{9,8},{10,9... | collective-permute-start | bytes 221192 | tf_op jit(solution)/shard_map/ppermute | solution.py:345
  58.7 1.2 %collective-permute-start.13 = (bf16[288,128]{1,0:T(8,128)(2,1)S(1)}, bf16[288,128]{1,0:T(8,128)(2,1)S(1)}, u32[]{:S(2)}, u32[]{:S(2)}) collective-permute-start(bf16[288,128]{1,0:T(8,128)(2,1)S(1)} %get-tuple-element.22), channel_id=1, source_target_pairs={{0,14},{1,15},{2,0},{3,1},{4,2},{5,3},{6,4},{7,5},{8,6},{9,7},{10,... | collective-permute-start | bytes 221192 | tf_op jit(solution)/shard_map/ppermute | solution.py:345
  59.9 0.8 %collective-permute-done.12.refs_0_ = bf16[288,128]{1,0:T(8,128)(2,1)S(1)} collective-permute-done((bf16[288,128]{1,0:T(8,128)(2,1)S(1)}, bf16[288,128]{1,0:T(8,128)(2,1)S(1)}, u32[]{:S(2)}, u32[]{:S(2)}) %collective-permute-start.12) | collective-permute-done | bytes 73760 | tf_op jit(solution)/shard_map/ppermute | solution.py:345
  60.7 2.5 %collective-permute-done.13.refs_1_ = bf16[288,128]{1,0:T(8,128)(2,1)S(1)} collective-permute-done((bf16[288,128]{1,0:T(8,128)(2,1)S(1)}, bf16[288,128]{1,0:T(8,128)(2,1)S(1)}, u32[]{:S(2)}, u32[]{:S(2)}) %collective-permute-start.13) | collective-permute-done | bytes 73760 | tf_op jit(solution)/shard_map/ppermute | solution.py:345
  63.2 0.6 collective-permute-done.14.refs_2_
  63.8 1.2 %join.1 = bf16[7,144,2,128]{3,2,1,0:T(2,128)(2,1)} custom-call(f32[4,288,128]{2,1,0:T(8,128)S(1)} %get-tuple-element.19.behind_ref, f32[4,288,128]{2,1,0:T(8,128)S(1)} %get-tuple-element.20.ahead_ref, bf16[288,128]{1,0:T(8,128)(2,1)S(1)} %collective-permute-done.12.refs_0_, bf16[288,128]{1,0:T(8,128)(2,1)S(1)} %collective-permute-done.13.refs_1_, ...), custom_call_target="tpu_custom_call" | custom-call | tf_op jit(solution)/shard_map/join/pallas_call | solution.py:317
  (17 shorter events, 0.1 us)
Async XLA Ops:
  2.8 15.0 %collective-permute-start.10 = (bf16[12,128,128]{2,1,0:T(8,128)(2,1)S(1)}, bf16[12,128,128]{2,1,0:T(8,128)(2,1)S(1)}, u32[]{:S(2)}, u32[]{:S(2)}) collective-permute-start(bf16[12,128,128]{2,1,0:T(8,128)(2,1)S(1)} %whiten_hour.5.refs_0_), channel_id=1, source_target_pairs={{15,13},{11,9},{7,5},{3,1},{14,12},{10,8},{6,4},{2,0},{13,10},{9,6... | collective-permute-start | bytes 1179656 | tf_op jit(solution)/shard_map/ppermute | solution.py:340
  8.3 20.7 %collective-permute-start.9 = (bf16[12,128,128]{2,1,0:T(8,128)(2,1)S(1)}, bf16[12,128,128]{2,1,0:T(8,128)(2,1)S(1)}, u32[]{:S(2)}, u32[]{:S(2)}) collective-permute-start(bf16[12,128,128]{2,1,0:T(8,128)(2,1)S(1)} %whiten_hour.5.refs_0_), channel_id=1, source_target_pairs={{15,14},{11,10},{7,6},{3,2},{13,12},{9,8},{5,4},{1,0},{14,11},{10,... | collective-permute-start | bytes 1179656 | tf_op jit(solution)/shard_map/ppermute | solution.py:340
  9.6 22.2 %collective-permute-start.7 = (bf16[12,128,128]{2,1,0:T(8,128)(2,1)S(1)}, bf16[12,128,128]{2,1,0:T(8,128)(2,1)S(1)}, u32[]{:S(2)}, u32[]{:S(2)}) collective-permute-start(bf16[12,128,128]{2,1,0:T(8,128)(2,1)S(1)} %whiten_hour.4.refs_0_), channel_id=1, source_target_pairs={{15,13},{11,9},{7,5},{3,1},{14,12},{10,8},{6,4},{2,0},{13,10},{9,6... | collective-permute-start | bytes 1179656 | tf_op jit(solution)/shard_map/ppermute | solution.py:340
  10.1 22.5 %collective-permute-start.4 = (bf16[12,128,128]{2,1,0:T(8,128)(2,1)S(1)}, bf16[12,128,128]{2,1,0:T(8,128)(2,1)S(1)}, u32[]{:S(2)}, u32[]{:S(2)}) collective-permute-start(bf16[12,128,128]{2,1,0:T(8,128)(2,1)S(1)} %get-tuple-element.18.refs_0_), channel_id=1, source_target_pairs={{0,2},{4,6},{8,10},{12,14},{1,3},{5,7},{9,11},{13,15},{2,5},{6,9},... | collective-permute-start | bytes 1179656 | tf_op jit(solution)/shard_map/ppermute | solution.py:340
  17.8 14.8 %collective-permute-start.11 = (bf16[12,128,128]{2,1,0:T(8,128)(2,1)S(1)}, bf16[12,128,128]{2,1,0:T(8,128)(2,1)S(1)}, u32[]{:S(2)}, u32[]{:S(2)}) collective-permute-start(bf16[12,128,128]{2,1,0:T(8,128)(2,1)S(1)} %collective-permute-done.10.refs_2_), channel_id=1, source_target_pairs={{15,14},{11,10},{7,6},{3,2},{14,15},{10,11},{6,7},{2,3},{13,12},{9... | collective-permute-start | bytes 1179656 | tf_op jit(solution)/shard_map/ppermute | solution.py:340
  17.9 20.4 %collective-permute-start.6 = (bf16[12,128,128]{2,1,0:T(8,128)(2,1)S(1)}, bf16[12,128,128]{2,1,0:T(8,128)(2,1)S(1)}, u32[]{:S(2)}, u32[]{:S(2)}) collective-permute-start(bf16[12,128,128]{2,1,0:T(8,128)(2,1)S(1)} %whiten_hour.4.refs_0_), channel_id=1, source_target_pairs={{15,14},{11,10},{7,6},{3,2},{13,12},{9,8},{5,4},{1,0},{14,11},{10,... | collective-permute-start | bytes 1179656 | tf_op jit(solution)/shard_map/ppermute | solution.py:340
  29.0 13.1 %collective-permute-start.1 = (bf16[12,128,128]{2,1,0:T(8,128)(2,1)S(1)}, bf16[12,128,128]{2,1,0:T(8,128)(2,1)S(1)}, u32[]{:S(2)}, u32[]{:S(2)}) collective-permute-start(bf16[12,128,128]{2,1,0:T(8,128)(2,1)S(1)} %whiten_hour.3.refs_0_), channel_id=1, source_target_pairs={{0,2},{4,6},{8,10},{12,14},{1,3},{5,7},{9,11},{13,15},{2,5},{6,9},... | collective-permute-start | bytes 1179656 | tf_op jit(solution)/shard_map/ppermute | solution.py:340
  31.8 10.3 %collective-permute-start.8 = (bf16[12,128,128]{2,1,0:T(8,128)(2,1)S(1)}, bf16[12,128,128]{2,1,0:T(8,128)(2,1)S(1)}, u32[]{:S(2)}, u32[]{:S(2)}) collective-permute-start(bf16[12,128,128]{2,1,0:T(8,128)(2,1)S(1)} %collective-permute-done.7.refs_2_), channel_id=1, source_target_pairs={{15,14},{11,10},{7,6},{3,2},{14,15},{10,11},{6,7},{2,3},{13,12},{9... | collective-permute-start | bytes 1179656 | tf_op jit(solution)/shard_map/ppermute | solution.py:340
  32.6 12.5 %collective-permute-start.3 = (bf16[12,128,128]{2,1,0:T(8,128)(2,1)S(1)}, bf16[12,128,128]{2,1,0:T(8,128)(2,1)S(1)}, u32[]{:S(2)}, u32[]{:S(2)}) collective-permute-start(bf16[12,128,128]{2,1,0:T(8,128)(2,1)S(1)} %get-tuple-element.18.refs_0_), channel_id=1, source_target_pairs={{0,1},{4,5},{8,9},{12,13},{2,3},{6,7},{10,11},{14,15},{1,4},{5,8},... | collective-permute-start | bytes 1179656 | tf_op jit(solution)/shard_map/ppermute | solution.py:340
  32.6 16.2 %collective-permute-start.5 = (bf16[12,128,128]{2,1,0:T(8,128)(2,1)S(1)}, bf16[12,128,128]{2,1,0:T(8,128)(2,1)S(1)}, u32[]{:S(2)}, u32[]{:S(2)}) collective-permute-start(bf16[12,128,128]{2,1,0:T(8,128)(2,1)S(1)} %collective-permute-done.4.refs_2_), channel_id=1, source_target_pairs={{0,1},{4,5},{8,9},{12,13},{1,0},{5,4},{9,8},{13,12},{2,3},{6,7},{1... | collective-permute-start | bytes 1179656 | tf_op jit(solution)/shard_map/ppermute | solution.py:340
  38.3 14.6 %collective-permute-start = (bf16[12,128,128]{2,1,0:T(8,128)(2,1)S(1)}, bf16[12,128,128]{2,1,0:T(8,128)(2,1)S(1)}, u32[]{:S(2)}, u32[]{:S(2)}) collective-permute-start(bf16[12,128,128]{2,1,0:T(8,128)(2,1)S(1)} %whiten_hour.3.refs_0_), channel_id=1, source_target_pairs={{0,1},{4,5},{8,9},{12,13},{2,3},{6,7},{10,11},{14,15},{1,4},{5,8},... | collective-permute-start | bytes 1179656 | tf_op jit(solution)/shard_map/ppermute | solution.py:340
  42.1 10.8 %collective-permute-start.2 = (bf16[12,128,128]{2,1,0:T(8,128)(2,1)S(1)}, bf16[12,128,128]{2,1,0:T(8,128)(2,1)S(1)}, u32[]{:S(2)}, u32[]{:S(2)}) collective-permute-start(bf16[12,128,128]{2,1,0:T(8,128)(2,1)S(1)} %collective-permute-done.1.refs_2_), channel_id=1, source_target_pairs={{0,1},{4,5},{8,9},{12,13},{1,0},{5,4},{9,8},{13,12},{2,3},{6,7},{1... | collective-permute-start | bytes 1179656 | tf_op jit(solution)/shard_map/ppermute | solution.py:340
  44.5 15.4 %collective-permute-start.15 = (bf16[288,128]{1,0:T(8,128)(2,1)S(1)}, bf16[288,128]{1,0:T(8,128)(2,1)S(1)}, u32[]{:S(2)}, u32[]{:S(2)}) collective-permute-start(bf16[288,128]{1,0:T(8,128)(2,1)S(1)} %get-tuple-element.24), channel_id=1, source_target_pairs={{0,1},{1,2},{2,3},{3,4},{4,5},{5,6},{6,7},{7,8},{8,9},{9,10},{10,1... | collective-permute-start | bytes 221192 | tf_op jit(solution)/shard_map/ppermute | solution.py:345
  45.1 14.8 %collective-permute-start.16 = (bf16[288,128]{1,0:T(8,128)(2,1)S(1)}, bf16[288,128]{1,0:T(8,128)(2,1)S(1)}, u32[]{:S(2)}, u32[]{:S(2)}) collective-permute-start(bf16[288,128]{1,0:T(8,128)(2,1)S(1)} %get-tuple-element.25), channel_id=1, source_target_pairs={{0,2},{1,3},{2,4},{3,5},{4,6},{5,7},{6,8},{7,9},{8,10},{9,11},{10,... | collective-permute-start | bytes 221192 | tf_op jit(solution)/shard_map/ppermute | solution.py:345
  48.9 11.0 %collective-permute-start.17 = (bf16[288,128]{1,0:T(8,128)(2,1)S(1)}, bf16[288,128]{1,0:T(8,128)(2,1)S(1)}, u32[]{:S(2)}, u32[]{:S(2)}) collective-permute-start(bf16[288,128]{1,0:T(8,128)(2,1)S(1)} %get-tuple-element.26), channel_id=1, source_target_pairs={{0,3},{1,4},{2,5},{3,6},{4,7},{5,8},{6,9},{7,10},{8,11},{9,12},{10... | collective-permute-start | bytes 221192 | tf_op jit(solution)/shard_map/ppermute | solution.py:345
  55.4 5.3 %collective-permute-start.12 = (bf16[288,128]{1,0:T(8,128)(2,1)S(1)}, bf16[288,128]{1,0:T(8,128)(2,1)S(1)}, u32[]{:S(2)}, u32[]{:S(2)}) collective-permute-start(bf16[288,128]{1,0:T(8,128)(2,1)S(1)} %get-tuple-element.21), channel_id=1, source_target_pairs={{0,15},{1,0},{2,1},{3,2},{4,3},{5,4},{6,5},{7,6},{8,7},{9,8},{10,9... | collective-permute-start | bytes 221192 | tf_op jit(solution)/shard_map/ppermute | solution.py:345
  58.7 4.5 %collective-permute-start.13 = (bf16[288,128]{1,0:T(8,128)(2,1)S(1)}, bf16[288,128]{1,0:T(8,128)(2,1)S(1)}, u32[]{:S(2)}, u32[]{:S(2)}) collective-permute-start(bf16[288,128]{1,0:T(8,128)(2,1)S(1)} %get-tuple-element.22), channel_id=1, source_target_pairs={{0,14},{1,15},{2,0},{3,1},{4,2},{5,3},{6,4},{7,5},{8,6},{9,7},{10,... | collective-permute-start | bytes 221192 | tf_op jit(solution)/shard_map/ppermute | solution.py:345
  59.9 4.0 %collective-permute-start.14 = (bf16[288,128]{1,0:T(8,128)(2,1)S(1)}, bf16[288,128]{1,0:T(8,128)(2,1)S(1)}, u32[]{:S(2)}, u32[]{:S(2)}) collective-permute-start(bf16[288,128]{1,0:T(8,128)(2,1)S(1)} %get-tuple-element.23), channel_id=1, source_target_pairs={{0,13},{1,14},{2,15},{3,0},{4,1},{5,2},{6,3},{7,4},{8,5},{9,6},{10... | collective-permute-start | bytes 221192 | tf_op jit(solution)/shard_map/ppermute | solution.py:345

commit v3 on v2

--- a/solution.py
+++ b/solution.py
@@ -2,6 +2,7 @@
 
 import jax
 import jax.numpy as jnp
+import numpy as np
 from jax import lax
 from jax.experimental import pallas as pl
 from jax.experimental.pallas import tpu as pltpu
@@ -24,14 +25,16 @@
 
 def fourier_matrix(samples):
     freq_bins = samples // 2
-    times_axis = jnp.arange(samples, dtype=jnp.int32)
-    bins_axis = jnp.arange(freq_bins, dtype=jnp.int32)
+    times_axis = np.arange(samples, dtype=np.int32)
+    bins_axis = np.arange(freq_bins, dtype=np.int32)
     phase_idx = times_axis[:, None] * bins_axis[None, :] % samples
-    angle = 2.0 * math.pi / samples * phase_idx.astype(jnp.float32)
-    taper = 0.5 - 0.5 * jnp.cos(2.0 * math.pi / samples * (times_axis.astype(jnp.float32) + 0.5))
-    table_re = taper[:, None] * jnp.cos(angle)
-    table_im = -taper[:, None] * jnp.sin(angle)
-    return jnp.concatenate([table_re.T, table_im.T], axis=0).astype(jnp.bfloat16)
+    step = np.float32(2.0 * math.pi / samples)
+    angle = step * phase_idx.astype(np.float32)
+    half = np.float32(0.5)
+    taper = half - half * np.cos(step * (times_axis.astype(np.float32) + half))
+    table_re = taper[:, None] * np.cos(angle)
+    table_im = -taper[:, None] * np.sin(angle)
+    return jnp.asarray(np.concatenate([table_re.T, table_im.T], axis=0).astype(jnp.bfloat16))
 
 
 def lane_iota(rows):
@@ -82,15 +85,21 @@
             out_ref[at] = value.astype(jnp.bfloat16)
 
 
-def whiten_first_kernel(counts_hbm, records_hbm, gap_hbm, table_ref, *refs):
-    out_ref, rest_ref, valid_ref, counts_ref, records_ref, gap_ref, sems = refs
+def whiten_first_kernel(counts_hbm, records_hbm, gap_hbm, table_hbm, *refs):
+    out_ref, rest_ref, valid_ref, table_ref, counts_ref, records_ref, gap_ref, sems = refs
     seg_hour = records_ref.shape[1]
     hours = valid_ref.shape[0]
 
     def hour_of(hour):
         return records_hbm.at[:, pl.ds(hour * seg_hour, seg_hour), :]
 
-    moves = [(counts_hbm, counts_ref), (gap_hbm, gap_ref), (hour_of(0), records_ref)]
+    moves = [
+        (counts_hbm, counts_ref),
+        (gap_hbm, gap_ref),
+        (table_hbm, table_ref),
+        (hour_of(0), records_ref),
+    ]
+    now = len(moves)
     moves += [(hour_of(hour), rest_ref.at[hour - 1]) for hour in range(1, hours)]
     copies = [
         pltpu.make_async_copy(source, target, sems.at[i])
@@ -98,14 +107,14 @@
     ]
     for copy in copies:
         copy.start()
-    for copy in copies[:3]:
+    for copy in copies[:now]:
         copy.wait()
     valid = [validity_rows(hour, seg_hour, counts_ref, gap_ref) for hour in range(hours)]
     for hour in range(1, hours):
         for station, row in enumerate(valid[hour]):
             valid_ref[hour, station : station + 1, :] = row
     whiten_block(records_ref, valid[0], table_ref, out_ref)
-    for copy in copies[3:]:
+    for copy in copies[now:]:
         copy.wait()
 
 
@@ -122,21 +131,24 @@
             jax.ShapeDtypeStruct((channels, samples // 2, LANES), jnp.bfloat16),
             jax.ShapeDtypeStruct((hours - 1, *block), records.dtype),
             jax.ShapeDtypeStruct((hours, stations, LANES), jnp.float32),
+            jax.ShapeDtypeStruct(table.shape, table.dtype),
         ],
-        in_specs=[hbm, hbm, hbm, vmem],
-        out_specs=[vmem] * 3,
+        in_specs=[hbm] * 4,
+        out_specs=[vmem] * 4,
         scratch_shapes=[
             pltpu.SMEM(counts.shape, counts.dtype),
             pltpu.VMEM(block, records.dtype),
             pltpu.VMEM(gap_mask.shape, gap_mask.dtype),
-            pltpu.SemaphoreType.DMA((hours + 2,)),
+            pltpu.SemaphoreType.DMA((hours + 3,)),
         ],
         cost_estimate=WHITEN_COST,
         compiler_params=pltpu.CompilerParams(vmem_limit_bytes=4 * MIB),
         name="whiten_first",
     )(
-        *(pltpu.with_memory_space_constraint(x, pltpu.HBM) for x in (counts, records, gap_mask)),
-        table,
+        *(
+            pltpu.with_memory_space_constraint(x, pltpu.HBM)
+            for x in (counts, records, gap_mask, table)
+        )
     )
 
 
@@ -377,7 +389,7 @@
     bins = samples // 2
     count = lax.axis_size("sta")
     table = fourier_matrix(samples)
-    first, rest, valid = whiten_first(records, counts, gap_mask, table)
+    first, rest, valid, table = whiten_first(records, counts, gap_mask, table)
     whitened = [first] + [whiten_hour(rest, valid, table, hour) for hour in range(1, hours)]
     partners = [fetch_partners(whitened[hour], count, hour) for hour in range(hours)]
     sums = [None, None]

time: 65.4 us -> 64.8 us (level)
  no operation moved by 1% of the time
where the time goes in v3:
time: 64.8 us; the launch traced here: 64.4 us
  starting transfers between devices  34.5 us (53%)
  waiting for transfers between devices  17.4 us (27%)
  Pallas kernels  12.4 us (19%)
    ppermute x12, starting transfers between devices, send(): return lax.ppermute(value, 'sta', pairs)  23.2 us
    ppermute x12, waiting for transfers between devices, send(): return lax.ppermute(value, 'sta', pairs)  13.5 us
    ppermute x6, starting transfers between devices, shift(): return lax.ppermute(value, 'sta', pairs)  11.3 us
    pallas_call x4, Pallas kernels, pair_hour(): pl.pallas_call(lambda *refs: pair_hour_kernel(hours, first, last, mirrore...  7.99 us
    ppermute x6, waiting for transfers between devices, shift(): return lax.ppermute(value, 'sta', pairs)  3.95 us
    pallas_call x1, Pallas kernels, whiten_first(): pl.pallas_call(whiten_first_kernel, out_shape=[jax.ShapeDtypeStruct((chan...  1.66 us
    pallas_call x3, Pallas kernels, whiten_hour(): pl.pallas_call(lambda *refs: whiten_hour_kernel(hour, *refs), out_shape=j...  1.53 us
  transfers between devices with their start and end apart: 18, of which 7 were waited for; matrix products, arithmetic and copies ran while one was open for 0% of the time, Pallas kernels for 14%

profile of v3, /device:TPU:0, one launch (start us, length us, event | category | flops | bytes accessed | tf_op | source)
XLA Modules:
  0.0 64.4 jit_solution(135675415608760532)
XLA Ops:
  0.0 1.7 %whiten_first.1 = (bf16[12,128,128]{2,1,0:T(8,128)(2,1)S(1)}, bf16[3,12,64,256]{3,2,1,0:T(8,128)(2,1)S(1)}, f32[4,4,128]{2,1,0:T(4,128)S(1)}, bf16[256,256]{1,0:T(8,128)(2,1)S(1)}) custom-call(s32[4,4]{1,0:T(4,128)} %counts_hbm.1, bf16[12,256,256]{2,1,0:T(8,128)(2,1)} %records_hbm.1, s32[4,256]{1,0:T(4,128)} %gap_hbm.1, bf16[256,256]{1,0:T(8,128)(2,1)} %constant.2.clone.table_hbm), custom_call_target="tpu_custom_call" | custom-call | flops 2000000000 | bytes 8000000 | tf_op jit(solution)/shard_map/whiten_first/pallas_call | solution.py:128
  1.7 0.5 whiten_hour.5.refs_0_
  2.2 5.5 %collective-permute-start.10 = (bf16[12,128,128]{2,1,0:T(8,128)(2,1)S(1)}, bf16[12,128,128]{2,1,0:T(8,128)(2,1)S(1)}, u32[]{:S(2)}, u32[]{:S(2)}) collective-permute-start(bf16[12,128,128]{2,1,0:T(8,128)(2,1)S(1)} %whiten_hour.5.refs_0_), channel_id=1, source_target_pairs={{15,13},{11,9},{7,5},{3,1},{14,12},{10,8},{6,4},{2,0},{13,10},{9,6... | collective-permute-start | bytes 1179656 | tf_op jit(solution)/shard_map/ppermute | solution.py:352
  7.7 0.7 %collective-permute-start.9 = (bf16[12,128,128]{2,1,0:T(8,128)(2,1)S(1)}, bf16[12,128,128]{2,1,0:T(8,128)(2,1)S(1)}, u32[]{:S(2)}, u32[]{:S(2)}) collective-permute-start(bf16[12,128,128]{2,1,0:T(8,128)(2,1)S(1)} %whiten_hour.5.refs_0_), channel_id=1, source_target_pairs={{15,14},{11,10},{7,6},{3,2},{13,12},{9,8},{5,4},{1,0},{14,11},{10,... | collective-permute-start | bytes 1179656 | tf_op jit(solution)/shard_map/ppermute | solution.py:352
  8.5 0.5 whiten_hour.4.refs_0_
  9.0 0.5 collective-permute-start.7
  9.5 1.6 %collective-permute-start.4 = (bf16[12,128,128]{2,1,0:T(8,128)(2,1)S(1)}, bf16[12,128,128]{2,1,0:T(8,128)(2,1)S(1)}, u32[]{:S(2)}, u32[]{:S(2)}) collective-permute-start(bf16[12,128,128]{2,1,0:T(8,128)(2,1)S(1)} %get-tuple-element.20.refs_0_), channel_id=1, source_target_pairs={{0,2},{4,6},{8,10},{12,14},{1,3},{5,7},{9,11},{13,15},{2,5},{6,9},... | collective-permute-start | bytes 1179656 | tf_op jit(solution)/shard_map/ppermute | solution.py:352
  11.1 6.2 %collective-permute-done.10.refs_2_ = bf16[12,128,128]{2,1,0:T(8,128)(2,1)S(1)} collective-permute-done((bf16[12,128,128]{2,1,0:T(8,128)(2,1)S(1)}, bf16[12,128,128]{2,1,0:T(8,128)(2,1)S(1)}, u32[]{:S(2)}, u32[]{:S(2)}) %collective-permute-start.10) | collective-permute-done | bytes 393248 | tf_op jit(solution)/shard_map/ppermute | solution.py:352
  17.2 0.1 collective-permute-start.11
  17.3 10.5 %collective-permute-start.6 = (bf16[12,128,128]{2,1,0:T(8,128)(2,1)S(1)}, bf16[12,128,128]{2,1,0:T(8,128)(2,1)S(1)}, u32[]{:S(2)}, u32[]{:S(2)}) collective-permute-start(bf16[12,128,128]{2,1,0:T(8,128)(2,1)S(1)} %whiten_hour.4.refs_0_), channel_id=1, source_target_pairs={{15,14},{11,10},{7,6},{3,2},{13,12},{9,8},{5,4},{1,0},{14,11},{10,... | collective-permute-start | bytes 1179656 | tf_op jit(solution)/shard_map/ppermute | solution.py:352
  27.9 0.5 whiten_hour.3.refs_0_
  28.4 0.1 collective-permute-start.1
  28.5 2.8 %collective-permute-done.7.refs_2_ = bf16[12,128,128]{2,1,0:T(8,128)(2,1)S(1)} collective-permute-done((bf16[12,128,128]{2,1,0:T(8,128)(2,1)S(1)}, bf16[12,128,128]{2,1,0:T(8,128)(2,1)S(1)}, u32[]{:S(2)}, u32[]{:S(2)}) %collective-permute-start.7) | collective-permute-done | bytes 393248 | tf_op jit(solution)/shard_map/ppermute | solution.py:352
  31.2 0.8 %collective-permute-done.4.refs_2_ = bf16[12,128,128]{2,1,0:T(8,128)(2,1)S(1)} collective-permute-done((bf16[12,128,128]{2,1,0:T(8,128)(2,1)S(1)}, bf16[12,128,128]{2,1,0:T(8,128)(2,1)S(1)}, u32[]{:S(2)}, u32[]{:S(2)}) %collective-permute-start.4) | collective-permute-done | bytes 393248 | tf_op jit(solution)/shard_map/ppermute | solution.py:352
  32.0 0.0 collective-permute-done.11.refs_3_
  32.0 4.1 %collective-permute-start.5 = (bf16[12,128,128]{2,1,0:T(8,128)(2,1)S(1)}, bf16[12,128,128]{2,1,0:T(8,128)(2,1)S(1)}, u32[]{:S(2)}, u32[]{:S(2)}) collective-permute-start(bf16[12,128,128]{2,1,0:T(8,128)(2,1)S(1)} %collective-permute-done.4.refs_2_), channel_id=1, source_target_pairs={{0,1},{4,5},{8,9},{12,13},{1,0},{5,4},{9,8},{13,12},{2,3},{6,7},{1... | collective-permute-start | bytes 1179656 | tf_op jit(solution)/shard_map/ppermute | solution.py:352
  36.1 1.6 %pair_hour.3.refs_4_ = f32[2048,128]{1,0:T(8,128)S(1)} custom-call(bf16[12,128,128]{2,1,0:T(8,128)(2,1)S(1)} %whiten_hour.5.refs_0_, bf16[12,128,128]{2,1,0:T(8,128)(2,1)S(1)} %collective-permute-done.9.refs_1_, bf16[12,128,128]{2,1,0:T(8,128)(2,1)S(1)} %collective-permute-done.10.refs_2_, bf16[12,128,128]{2,1,0:T(8,128)(2,1)S(1)} %collective-permute-done.11.refs_3_), custom_call_target="tpu_custom_call" | custom-call | flops 3000000000 | bytes 12000000 | tf_op jit(solution)/shard_map/pair_hour/pallas_call | solution.py:301
  37.7 0.1 collective-permute-start
  37.7 3.7 %collective-permute-done.1.refs_2_ = bf16[12,128,128]{2,1,0:T(8,128)(2,1)S(1)} collective-permute-done((bf16[12,128,128]{2,1,0:T(8,128)(2,1)S(1)}, bf16[12,128,128]{2,1,0:T(8,128)(2,1)S(1)}, u32[]{:S(2)}, u32[]{:S(2)}) %collective-permute-start.1) | collective-permute-done | bytes 393248 | tf_op jit(solution)/shard_map/ppermute | solution.py:352
  41.5 2.4 %pair_hour_last.3 = (f32[4,288,128]{2,1,0:T(8,128)S(1)}, bf16[288,128]{1,0:T(8,128)(2,1)S(1)}, bf16[288,128]{1,0:T(8,128)(2,1)S(1)}, bf16[288,128]{1,0:T(8,128)(2,1)S(1)}) custom-call(bf16[12,128,128]{2,1,0:T(8,128)(2,1)S(1)} %whiten_hour.4.refs_0_, bf16[12,128,128]{2,1,0:T(8,128)(2,1)S(1)} %collective-permute-done.6.refs_1_, ...), custom_call_target="tpu_custom_call" | custom-call | flops 3000000000 | bytes 12000000 | tf_op jit(solution)/shard_map/pair_hour_last/pallas_call | solution.py:301
  43.9 0.6 collective-permute-start.15
  44.5 3.8 %collective-permute-start.16 = (bf16[288,128]{1,0:T(8,128)(2,1)S(1)}, bf16[288,128]{1,0:T(8,128)(2,1)S(1)}, u32[]{:S(2)}, u32[]{:S(2)}) collective-permute-start(bf16[288,128]{1,0:T(8,128)(2,1)S(1)} %get-tuple-element.27), channel_id=1, source_target_pairs={{0,2},{1,3},{2,4},{3,5},{4,6},{5,7},{6,8},{7,9},{8,10},{9,11},{10,... | collective-permute-start | bytes 221192 | tf_op jit(solution)/shard_map/ppermute | solution.py:357
  48.3 2.5 %collective-permute-start.17 = (bf16[288,128]{1,0:T(8,128)(2,1)S(1)}, bf16[288,128]{1,0:T(8,128)(2,1)S(1)}, u32[]{:S(2)}, u32[]{:S(2)}) collective-permute-start(bf16[288,128]{1,0:T(8,128)(2,1)S(1)} %get-tuple-element.28), channel_id=1, source_target_pairs={{0,3},{1,4},{2,5},{3,6},{4,7},{5,8},{6,9},{7,10},{8,11},{9,12},{10... | collective-permute-start | bytes 221192 | tf_op jit(solution)/shard_map/ppermute | solution.py:357
  50.8 1.5 %pair_hour.2.refs_4_ = f32[2048,128]{1,0:T(8,128)S(1)} custom-call(bf16[12,128,128]{2,1,0:T(8,128)(2,1)S(1)} %get-tuple-element.20.refs_0_, bf16[12,128,128]{2,1,0:T(8,128)(2,1)S(1)} %collective-permute-done.3.refs_1_, bf16[12,128,128]{2,1,0:T(8,128)(2,1)S(1)} %collective-permute-done.4.refs_2_, bf16[12,128,128]{2,1,0:T(8,128)(2,1)S(1)} %collective-permute-done.5.refs_3_), custom_call_target="tpu_custom_call" | custom-call | flops 3000000000 | bytes 12000000 | tf_op jit(solution)/shard_map/pair_hour/pallas_call | solution.py:301
  52.3 0.0 collective-permute-done.2.refs_3_
  52.3 2.4 %pair_hour_last.2 = (f32[4,288,128]{2,1,0:T(8,128)S(1)}, bf16[288,128]{1,0:T(8,128)(2,1)S(1)}, bf16[288,128]{1,0:T(8,128)(2,1)S(1)}, bf16[288,128]{1,0:T(8,128)(2,1)S(1)}) custom-call(bf16[12,128,128]{2,1,0:T(8,128)(2,1)S(1)} %whiten_hour.3.refs_0_, bf16[12,128,128]{2,1,0:T(8,128)(2,1)S(1)} %collective-permute-done.refs_1_, ...), custom_call_target="tpu_custom_call" | custom-call | flops 3000000000 | bytes 12000000 | tf_op jit(solution)/shard_map/pair_hour_last/pallas_call | solution.py:301
  54.8 3.3 %collective-permute-start.12 = (bf16[288,128]{1,0:T(8,128)(2,1)S(1)}, bf16[288,128]{1,0:T(8,128)(2,1)S(1)}, u32[]{:S(2)}, u32[]{:S(2)}) collective-permute-start(bf16[288,128]{1,0:T(8,128)(2,1)S(1)} %get-tuple-element.23), channel_id=1, source_target_pairs={{0,15},{1,0},{2,1},{3,2},{4,3},{5,4},{6,5},{7,6},{8,7},{9,8},{10,9... | collective-permute-start | bytes 221192 | tf_op jit(solution)/shard_map/ppermute | solution.py:357
  58.1 1.2 %collective-permute-start.13 = (bf16[288,128]{1,0:T(8,128)(2,1)S(1)}, bf16[288,128]{1,0:T(8,128)(2,1)S(1)}, u32[]{:S(2)}, u32[]{:S(2)}) collective-permute-start(bf16[288,128]{1,0:T(8,128)(2,1)S(1)} %get-tuple-element.24), channel_id=1, source_target_pairs={{0,14},{1,15},{2,0},{3,1},{4,2},{5,3},{6,4},{7,5},{8,6},{9,7},{10,... | collective-permute-start | bytes 221192 | tf_op jit(solution)/shard_map/ppermute | solution.py:357
  59.3 0.8 %collective-permute-done.12.refs_0_ = bf16[288,128]{1,0:T(8,128)(2,1)S(1)} collective-permute-done((bf16[288,128]{1,0:T(8,128)(2,1)S(1)}, bf16[288,128]{1,0:T(8,128)(2,1)S(1)}, u32[]{:S(2)}, u32[]{:S(2)}) %collective-permute-start.12) | collective-permute-done | bytes 73760 | tf_op jit(solution)/shard_map/ppermute | solution.py:357
  60.1 2.5 %collective-permute-done.13.refs_1_ = bf16[288,128]{1,0:T(8,128)(2,1)S(1)} collective-permute-done((bf16[288,128]{1,0:T(8,128)(2,1)S(1)}, bf16[288,128]{1,0:T(8,128)(2,1)S(1)}, u32[]{:S(2)}, u32[]{:S(2)}) %collective-permute-start.13) | collective-permute-done | bytes 73760 | tf_op jit(solution)/shard_map/ppermute | solution.py:357
  62.6 0.6 collective-permute-done.14.refs_2_
  63.2 1.2 %join.1 = bf16[7,144,2,128]{3,2,1,0:T(2,128)(2,1)} custom-call(f32[4,288,128]{2,1,0:T(8,128)S(1)} %get-tuple-element.21.behind_ref, f32[4,288,128]{2,1,0:T(8,128)S(1)} %get-tuple-element.22.ahead_ref, bf16[288,128]{1,0:T(8,128)(2,1)S(1)} %collective-permute-done.12.refs_0_, bf16[288,128]{1,0:T(8,128)(2,1)S(1)} %collective-permute-done.13.refs_1_, ...), custom_call_target="tpu_custom_call" | custom-call | tf_op jit(solution)/shard_map/join/pallas_call | solution.py:329
  (13 shorter events, 0.0 us)
Async XLA Ops:
  2.2 15.0 %collective-permute-start.10 = (bf16[12,128,128]{2,1,0:T(8,128)(2,1)S(1)}, bf16[12,128,128]{2,1,0:T(8,128)(2,1)S(1)}, u32[]{:S(2)}, u32[]{:S(2)}) collective-permute-start(bf16[12,128,128]{2,1,0:T(8,128)(2,1)S(1)} %whiten_hour.5.refs_0_), channel_id=1, source_target_pairs={{15,13},{11,9},{7,5},{3,1},{14,12},{10,8},{6,4},{2,0},{13,10},{9,6... | collective-permute-start | bytes 1179656 | tf_op jit(solution)/shard_map/ppermute | solution.py:352
  7.7 20.7 %collective-permute-start.9 = (bf16[12,128,128]{2,1,0:T(8,128)(2,1)S(1)}, bf16[12,128,128]{2,1,0:T(8,128)(2,1)S(1)}, u32[]{:S(2)}, u32[]{:S(2)}) collective-permute-start(bf16[12,128,128]{2,1,0:T(8,128)(2,1)S(1)} %whiten_hour.5.refs_0_), channel_id=1, source_target_pairs={{15,14},{11,10},{7,6},{3,2},{13,12},{9,8},{5,4},{1,0},{14,11},{10,... | collective-permute-start | bytes 1179656 | tf_op jit(solution)/shard_map/ppermute | solution.py:352
  9.0 22.2 %collective-permute-start.7 = (bf16[12,128,128]{2,1,0:T(8,128)(2,1)S(1)}, bf16[12,128,128]{2,1,0:T(8,128)(2,1)S(1)}, u32[]{:S(2)}, u32[]{:S(2)}) collective-permute-start(bf16[12,128,128]{2,1,0:T(8,128)(2,1)S(1)} %whiten_hour.4.refs_0_), channel_id=1, source_target_pairs={{15,13},{11,9},{7,5},{3,1},{14,12},{10,8},{6,4},{2,0},{13,10},{9,6... | collective-permute-start | bytes 1179656 | tf_op jit(solution)/shard_map/ppermute | solution.py:352
  9.5 22.5 %collective-permute-start.4 = (bf16[12,128,128]{2,1,0:T(8,128)(2,1)S(1)}, bf16[12,128,128]{2,1,0:T(8,128)(2,1)S(1)}, u32[]{:S(2)}, u32[]{:S(2)}) collective-permute-start(bf16[12,128,128]{2,1,0:T(8,128)(2,1)S(1)} %get-tuple-element.20.refs_0_), channel_id=1, source_target_pairs={{0,2},{4,6},{8,10},{12,14},{1,3},{5,7},{9,11},{13,15},{2,5},{6,9},... | collective-permute-start | bytes 1179656 | tf_op jit(solution)/shard_map/ppermute | solution.py:352
  17.2 14.8 %collective-permute-start.11 = (bf16[12,128,128]{2,1,0:T(8,128)(2,1)S(1)}, bf16[12,128,128]{2,1,0:T(8,128)(2,1)S(1)}, u32[]{:S(2)}, u32[]{:S(2)}) collective-permute-start(bf16[12,128,128]{2,1,0:T(8,128)(2,1)S(1)} %collective-permute-done.10.refs_2_), channel_id=1, source_target_pairs={{15,14},{11,10},{7,6},{3,2},{14,15},{10,11},{6,7},{2,3},{13,12},{9... | collective-permute-start | bytes 1179656 | tf_op jit(solution)/shard_map/ppermute | solution.py:352
  17.3 20.4 %collective-permute-start.6 = (bf16[12,128,128]{2,1,0:T(8,128)(2,1)S(1)}, bf16[12,128,128]{2,1,0:T(8,128)(2,1)S(1)}, u32[]{:S(2)}, u32[]{:S(2)}) collective-permute-start(bf16[12,128,128]{2,1,0:T(8,128)(2,1)S(1)} %whiten_hour.4.refs_0_), channel_id=1, source_target_pairs={{15,14},{11,10},{7,6},{3,2},{13,12},{9,8},{5,4},{1,0},{14,11},{10,... | collective-permute-start | bytes 1179656 | tf_op jit(solution)/shard_map/ppermute | solution.py:352
  28.4 13.1 %collective-permute-start.1 = (bf16[12,128,128]{2,1,0:T(8,128)(2,1)S(1)}, bf16[12,128,128]{2,1,0:T(8,128)(2,1)S(1)}, u32[]{:S(2)}, u32[]{:S(2)}) collective-permute-start(bf16[12,128,128]{2,1,0:T(8,128)(2,1)S(1)} %whiten_hour.3.refs_0_), channel_id=1, source_target_pairs={{0,2},{4,6},{8,10},{12,14},{1,3},{5,7},{9,11},{13,15},{2,5},{6,9},... | collective-permute-start | bytes 1179656 | tf_op jit(solution)/shard_map/ppermute | solution.py:352
  31.2 10.3 %collective-permute-start.8 = (bf16[12,128,128]{2,1,0:T(8,128)(2,1)S(1)}, bf16[12,128,128]{2,1,0:T(8,128)(2,1)S(1)}, u32[]{:S(2)}, u32[]{:S(2)}) collective-permute-start(bf16[12,128,128]{2,1,0:T(8,128)(2,1)S(1)} %collective-permute-done.7.refs_2_), channel_id=1, source_target_pairs={{15,14},{11,10},{7,6},{3,2},{14,15},{10,11},{6,7},{2,3},{13,12},{9... | collective-permute-start | bytes 1179656 | tf_op jit(solution)/shard_map/ppermute | solution.py:352
  32.0 12.5 %collective-permute-start.3 = (bf16[12,128,128]{2,1,0:T(8,128)(2,1)S(1)}, bf16[12,128,128]{2,1,0:T(8,128)(2,1)S(1)}, u32[]{:S(2)}, u32[]{:S(2)}) collective-permute-start(bf16[12,128,128]{2,1,0:T(8,128)(2,1)S(1)} %get-tuple-element.20.refs_0_), channel_id=1, source_target_pairs={{0,1},{4,5},{8,9},{12,13},{2,3},{6,7},{10,11},{14,15},{1,4},{5,8},... | collective-permute-start | bytes 1179656 | tf_op jit(solution)/shard_map/ppermute | solution.py:352
  32.0 16.3 %collective-permute-start.5 = (bf16[12,128,128]{2,1,0:T(8,128)(2,1)S(1)}, bf16[12,128,128]{2,1,0:T(8,128)(2,1)S(1)}, u32[]{:S(2)}, u32[]{:S(2)}) collective-permute-start(bf16[12,128,128]{2,1,0:T(8,128)(2,1)S(1)} %collective-permute-done.4.refs_2_), channel_id=1, source_target_pairs={{0,1},{4,5},{8,9},{12,13},{1,0},{5,4},{9,8},{13,12},{2,3},{6,7},{1... | collective-permute-start | bytes 1179656 | tf_op jit(solution)/shard_map/ppermute | solution.py:352
  37.7 14.6 %collective-permute-start = (bf16[12,128,128]{2,1,0:T(8,128)(2,1)S(1)}, bf16[12,128,128]{2,1,0:T(8,128)(2,1)S(1)}, u32[]{:S(2)}, u32[]{:S(2)}) collective-permute-start(bf16[12,128,128]{2,1,0:T(8,128)(2,1)S(1)} %whiten_hour.3.refs_0_), channel_id=1, source_target_pairs={{0,1},{4,5},{8,9},{12,13},{2,3},{6,7},{10,11},{14,15},{1,4},{5,8},... | collective-permute-start | bytes 1179656 | tf_op jit(solution)/shard_map/ppermute | solution.py:352
  41.5 10.8 %collective-permute-start.2 = (bf16[12,128,128]{2,1,0:T(8,128)(2,1)S(1)}, bf16[12,128,128]{2,1,0:T(8,128)(2,1)S(1)}, u32[]{:S(2)}, u32[]{:S(2)}) collective-permute-start(bf16[12,128,128]{2,1,0:T(8,128)(2,1)S(1)} %collective-permute-done.1.refs_2_), channel_id=1, source_target_pairs={{0,1},{4,5},{8,9},{12,13},{1,0},{5,4},{9,8},{13,12},{2,3},{6,7},{1... | collective-permute-start | bytes 1179656 | tf_op jit(solution)/shard_map/ppermute | solution.py:352
  43.9 15.4 %collective-permute-start.15 = (bf16[288,128]{1,0:T(8,128)(2,1)S(1)}, bf16[288,128]{1,0:T(8,128)(2,1)S(1)}, u32[]{:S(2)}, u32[]{:S(2)}) collective-permute-start(bf16[288,128]{1,0:T(8,128)(2,1)S(1)} %get-tuple-element.26), channel_id=1, source_target_pairs={{0,1},{1,2},{2,3},{3,4},{4,5},{5,6},{6,7},{7,8},{8,9},{9,10},{10,1... | collective-permute-start | bytes 221192 | tf_op jit(solution)/shard_map/ppermute | solution.py:357
  44.5 14.8 %collective-permute-start.16 = (bf16[288,128]{1,0:T(8,128)(2,1)S(1)}, bf16[288,128]{1,0:T(8,128)(2,1)S(1)}, u32[]{:S(2)}, u32[]{:S(2)}) collective-permute-start(bf16[288,128]{1,0:T(8,128)(2,1)S(1)} %get-tuple-element.27), channel_id=1, source_target_pairs={{0,2},{1,3},{2,4},{3,5},{4,6},{5,7},{6,8},{7,9},{8,10},{9,11},{10,... | collective-permute-start | bytes 221192 | tf_op jit(solution)/shard_map/ppermute | solution.py:357
  48.3 11.0 %collective-permute-start.17 = (bf16[288,128]{1,0:T(8,128)(2,1)S(1)}, bf16[288,128]{1,0:T(8,128)(2,1)S(1)}, u32[]{:S(2)}, u32[]{:S(2)}) collective-permute-start(bf16[288,128]{1,0:T(8,128)(2,1)S(1)} %get-tuple-element.28), channel_id=1, source_target_pairs={{0,3},{1,4},{2,5},{3,6},{4,7},{5,8},{6,9},{7,10},{8,11},{9,12},{10... | collective-permute-start | bytes 221192 | tf_op jit(solution)/shard_map/ppermute | solution.py:357
  54.8 5.3 %collective-permute-start.12 = (bf16[288,128]{1,0:T(8,128)(2,1)S(1)}, bf16[288,128]{1,0:T(8,128)(2,1)S(1)}, u32[]{:S(2)}, u32[]{:S(2)}) collective-permute-start(bf16[288,128]{1,0:T(8,128)(2,1)S(1)} %get-tuple-element.23), channel_id=1, source_target_pairs={{0,15},{1,0},{2,1},{3,2},{4,3},{5,4},{6,5},{7,6},{8,7},{9,8},{10,9... | collective-permute-start | bytes 221192 | tf_op jit(solution)/shard_map/ppermute | solution.py:357
  58.1 4.5 %collective-permute-start.13 = (bf16[288,128]{1,0:T(8,128)(2,1)S(1)}, bf16[288,128]{1,0:T(8,128)(2,1)S(1)}, u32[]{:S(2)}, u32[]{:S(2)}) collective-permute-start(bf16[288,128]{1,0:T(8,128)(2,1)S(1)} %get-tuple-element.24), channel_id=1, source_target_pairs={{0,14},{1,15},{2,0},{3,1},{4,2},{5,3},{6,4},{7,5},{8,6},{9,7},{10,... | collective-permute-start | bytes 221192 | tf_op jit(solution)/shard_map/ppermute | solution.py:357
  59.3 4.0 %collective-permute-start.14 = (bf16[288,128]{1,0:T(8,128)(2,1)S(1)}, bf16[288,128]{1,0:T(8,128)(2,1)S(1)}, u32[]{:S(2)}, u32[]{:S(2)}) collective-permute-start(bf16[288,128]{1,0:T(8,128)(2,1)S(1)} %get-tuple-element.25), channel_id=1, source_target_pairs={{0,13},{1,14},{2,15},{3,0},{4,1},{5,2},{6,3},{7,4},{8,5},{9,6},{10... | collective-permute-start | bytes 221192 | tf_op jit(solution)/shard_map/ppermute | solution.py:357
